TPU v7x, 512 devices: a whole 4x8x8 slice. The times are simulated.
512 devices in a mesh: seq: 64 (over y, x, core), chan: 8 (over z).
Axes of the slice: x: 4, y: 8, z: 8, core: 2. Of those that a mesh axis runs over, the one named last changes fastest.
Arguments:
- inputs: bfloat16 [4096, 8192], P('chan', 'seq'), may hold values from -6 to 6
- grad_out: bfloat16 [4096, 8192], P('chan', 'seq'), may hold values from -0.0625 to 0.0625
- out_weight: float32 [4096, 64], P('chan'), may hold values from -0.75 to 0.75
- decay_rate: float32 [4096], P('chan'), may hold values from 6.1035156e-05 to 0.04
- frequency: float32 [64], replicated, may hold values from 0.00036621094 to 1.5
- phase_shift: float32 [64], replicated, may hold values from -3.140625 to 3.140625
- sketch_matrix: float32 [4096, 32], P('chan'), may hold values from -0.0014648438 to 0.0014648438
Outputs:
- grad_input: bfloat16 [4096, 8192], P('chan', 'seq')
- grad_filter: bfloat16 [4096, 8192], P('chan', 'seq')
- sketch: float32 [32, 64], replicated
All inputs are finite; a program needn't handle non-finite values.
Results may differ from a plain program's by a relative error of at most 0.005.
Values may be sent and summed in bfloat16 or wider, within the bound.
No kernel may reach another device: no remote copies, remote signals or barrier semaphores. Data moves between devices by JAX's collectives and lax.ppermute only.
A program may use at most 64 MiB of HBM per device.

v0:
```python
import math

import jax
import jax.numpy as jnp
from jax import lax
from jax.experimental import pallas as pl
from jax.experimental.pallas import tpu as pltpu
from jax.sharding import PartitionSpec as P

LANES = 128
GROUP = 4

highest = lax.Precision.HIGHEST


def slab_kernel(got_ref, filt_ref, turn_ref, wave_ref, fall_ref, flip_ref, out_ref, rev_u, rev_f, rows_g, rows_o, mix):
    blocks = got_ref.shape[0]
    chans = filt_ref.shape[0]
    f32, bf16 = jnp.float32, jnp.bfloat16
    pad = rev_u.shape[0] // chans
    gpad = rows_g.shape[0] // chans
    flip = flip_ref[...]
    rev_u[...] = jnp.zeros(rev_u.shape, f32)
    rev_f[...] = jnp.zeros(rev_f.shape, f32)
    rows_g[...] = jnp.zeros(rows_g.shape, f32)
    for c in range(chans):
        rev_f[c * pad : c * pad + blocks, :] = filt_ref[c]
    for t in range(blocks):
        tile = got_ref[t]
        turned = jnp.dot(tile, flip, preferred_element_type=f32)
        rev_u[pl.ds(blocks - 1 - t, chans, stride=pad), :] = turned[:chans]
        rows_g[pl.ds(t, chans, stride=gpad), :] = tile.astype(f32)[chans:]

    row_id = lax.broadcasted_iota(jnp.int32, (LANES, LANES), 0)
    lane_id = lax.broadcasted_iota(jnp.int32, (LANES, LANES), 1)
    own = (lane_id <= row_id).astype(f32)

    def rolled(c, d):
        row = jnp.broadcast_to(rows_g[pl.ds(c * gpad + d, 1), :], (LANES, LANES))
        return pltpu.roll(row, 1, 1, stride=1, stride_axis=0)

    def channel(c, carry):
        acc = [[jnp.zeros((16, LANES), f32) for _ in range(blocks // 16)] for _ in range(2)]
        here = rolled(c, 0)
        for d0 in range(0, blocks, GROUP):
            pieces = []
            for d in range(d0, d0 + GROUP):
                after = rolled(c, d + 1)
                pieces.append(jnp.where(own > 0.5, here, after).astype(bf16))
                here = after
            hank = jnp.concatenate(pieces, axis=0)
            count = -(-(d0 + GROUP) // 16)
            left = []
            for ref in (rev_f, rev_u):
                left.append(
                    jnp.concatenate(
                        [
                            ref[pl.ds(c * pad + blocks - 1 - d, 16 * count), :].astype(bf16)
                            for d in range(d0, d0 + GROUP)
                        ],
                        axis=1,
                    )
                )
            res = jnp.dot(jnp.concatenate(left, axis=0), hank, preferred_element_type=f32)
            for s in range(2):
                for n in range(count):
                    at = (s * count + n) * 16
                    acc[s][n] = acc[s][n] + res[at : at + 16]
        grad_in = jnp.concatenate(acc[0], axis=0)
        grad_h = jnp.concatenate(acc[1], axis=0)
        rows_o[pl.ds(c, blocks, stride=2 * chans), :] = grad_in
        rows_o[pl.ds(c + chans, blocks, stride=2 * chans), :] = grad_h
        kept = grad_h.astype(bf16).astype(f32) * fall_ref[pl.ds(c, 1), :]
        spun = jnp.dot(kept, wave_ref[...], precision=highest, preferred_element_type=f32)
        mix[pl.ds(c, 1), :] = jnp.sum(spun * turn_ref[c], axis=0, keepdims=True)
        return carry

    lax.fori_loop(0, chans, channel, 0)
    total = mix[...]
    total = total + pltpu.roll(total, LANES // 2, 1)
    high = total.astype(bf16).astype(f32)
    lanes = lax.broadcasted_iota(jnp.int32, total.shape, 1)
    pair = jnp.where(lanes < LANES // 2, high, total - high).astype(bf16)
    for t in range(blocks):
        out_ref[t, : 2 * chans, :] = rows_o[2 * chans * t : 2 * chans * (t + 1), :].astype(bf16)
        out_ref[t, 2 * chans :, :] = pair


def run_slab(got, filt, turn, wave, fall, flip, interpret=False):
    blocks, rows, _ = got.shape
    chans = rows // 2
    f32 = jnp.float32
    return pl.pallas_call(
        slab_kernel,
        out_shape=jax.ShapeDtypeStruct((blocks, 3 * chans, LANES), jnp.bfloat16),
        scratch_shapes=[
            pltpu.VMEM((chans * 2 * blocks, LANES), f32),
            pltpu.VMEM((chans * 2 * blocks, LANES), f32),
            pltpu.VMEM((chans * (blocks + 8), LANES), f32),
            pltpu.VMEM((2 * chans * blocks, LANES), f32),
            pltpu.VMEM((chans, LANES), f32),
        ],
        compiler_params=pltpu.CompilerParams(vmem_limit_bytes=32 << 20),
        interpret=interpret,
    )(got, filt, turn, wave, fall, flip)


def filter_tables(weights, rates, frequency, phase_shift, blocks):
    hi = (LANES * jnp.arange(blocks)).astype(jnp.float32)
    lo = jnp.arange(LANES).astype(jnp.float32)
    outer = frequency[None, :] * hi[:, None] + phase_shift[None, :]
    inner = frequency[:, None] * lo[None, :]
    turn = jnp.concatenate([jnp.sin(outer), jnp.cos(outer)], axis=1)
    wave = jnp.concatenate([jnp.cos(inner), jnp.sin(inner)], axis=0)
    turn = jnp.exp(-rates[:, None] * hi[None, :])[:, :, None] * turn[None]
    fall = jnp.exp(-rates[:, None] * lo[None, :])
    both = jnp.concatenate([weights, weights], axis=1)
    mixed = jnp.einsum("ckj,jl->ckl", (turn * both[:, None, :])[:, ::-1], wave[:, ::-1], precision=highest)
    filt = mixed * fall[:, None, ::-1]
    return filt, turn, wave.T, fall


def per_device(inputs, grad_out, out_weight, decay_rate, frequency, phase_shift, sketch_matrix):
    groups = lax.axis_size("seq")
    parts = lax.axis_size("chan")
    seq_index = lax.axis_index("seq")
    width_local, tok_len = inputs.shape
    chans = width_local // groups
    order = frequency.shape[0]
    first_row = seq_index * chans
    sent = jnp.concatenate(
        [inputs.reshape(groups, chans, tok_len), grad_out.reshape(groups, chans, tok_len)], axis=1
    )
    got = lax.all_to_all(sent, "seq", split_axis=0, concat_axis=0, tiled=True)
    rates = lax.dynamic_slice_in_dim(decay_rate, first_row, chans, 0)
    weights = lax.dynamic_slice_in_dim(out_weight, first_row, chans, 0)
    filt, turn, wave, fall = filter_tables(weights, rates, frequency, phase_shift, groups)
    flip = jnp.eye(LANES, dtype=jnp.bfloat16)[::-1]
    back = run_slab(got, filt, turn, wave, fall, flip)
    home = lax.all_to_all(back, "seq", split_axis=0, concat_axis=0, tiled=True)
    pair = home[:, 2 * chans :, :].astype(jnp.float32)
    grad_mix = (pair[:, :, :order] + pair[:, :, order:]).reshape(width_local, order)
    partial_sum = jnp.dot(sketch_matrix.T, grad_mix, precision=highest, preferred_element_type=jnp.float32)
    everyone = jnp.broadcast_to(partial_sum[None], (parts, *partial_sum.shape))
    sketch = jnp.sum(lax.all_to_all(everyone, "chan", split_axis=0, concat_axis=0, tiled=True), axis=0)
    grad_in = home[:, :chans, :].reshape(width_local, tok_len)
    grad_h = home[:, chans : 2 * chans, :].reshape(width_local, tok_len)
    return (grad_in, grad_h, sketch)


def solution(mesh):
    placed = (
        P("chan", "seq"),
        P("chan", "seq"),
        P("chan", None),
        P("chan"),
        P(),
        P(),
        P("chan", None),
    )
    return jax.shard_map(
        per_device,
        mesh=mesh,
        in_specs=placed,
        out_specs=(P("chan", "seq"), P("chan", "seq"), P()),
        check_vma=False,
    )
```

profile of v0, /device:TPU:16, one launch (start us, length us, event | category | flops | bytes accessed | tf_op | source)
XLA Modules:
  0.0 76.6 jit_solution(3590783440549743334)
XLA Ops:
  0.6 0.0 copy-start
  0.6 1.7 %pad_maximum_fusion = bf16[64,16,128]{2,1,0:T(8,128)(2,1)} fusion(bf16[64,8,128]{2,1,0:T(8,128)(2,1)} %bitcast.18, bf16[64,8,128]{2,1,0:T(8,128)(2,1)} %bitcast.19), kind=kLoop, calls=%fused_computation.5 | loop fusion | flops 524288 | bytes 524288 | tf_op jit(solution)/shard_map/concatenate | solution.py:131
  2.4 10.5 %all-to-all-start = ((bf16[64,16,128]{2,1,0:T(8,128)(2,1)}), bf16[64,16,128]{2,1,0:T(8,128)(2,1)S(1)}, u32[]{:S(2)}, u32[]{:S(2)}) async-start(bf16[64,16,128]{2,1,0:T(8,128)(2,1)} %pad_maximum_fusion), calls=%async_computation | async-start | bytes 524288 | tf_op jit(solution)/shard_map/all_to_all | solution.py:134
  12.9 0.8 dynamic-slice_negate_fusion
  13.6 0.0 copy-done
  13.6 0.1 constant_dynamic-slice_fusion
  13.7 0.1 copy.18
  13.8 0.1 pad_maximum_fusion.3
  13.9 0.1 multiply_exponential_fusion.1
  13.9 0.0 copy-start.2
  13.9 0.1 multiply_exponential_fusion.fall_ref
  14.0 0.6 copy-done.2
  14.6 0.0 copy-start.3
  14.6 0.3 multiply_cosine_fusion
  14.9 0.3 copy-done.3
  15.3 0.2 fusion.6
  15.5 0.1 pad_maximum_fusion.2
  15.5 0.1 broadcast_multiply_fusion.1
  15.7 0.1 pad_maximum_fusion.1
  15.8 0.1 rev.14
  16.0 0.1 fusion.9.wave_ref
  16.0 0.4 convolution_multiply_fusion.filt_ref
  16.4 8.7 %all-to-all-done.got_ref = bf16[64,16,128]{2,1,0:T(8,128)(2,1)S(1)} async-done(((bf16[64,16,128]{2,1,0:T(8,128)(2,1)}), bf16[64,16,128]{2,1,0:T(8,128)(2,1)S(1)}, u32[]{:S(2)}, u32[]{:S(2)}) %all-to-all-start) | async-done | bytes 262176 | tf_op jit(solution)/shard_map/all_to_all | solution.py:134
  25.2 9.1 %shard_map.94 = bf16[64,24,128]{2,1,0:T(8,128)(2,1)S(1)} custom-call(bf16[64,16,128]{2,1,0:T(8,128)(2,1)S(1)} %all-to-all-done.got_ref, f32[8,64,128]{2,1,0:T(8,128)S(1)} %convolution_multiply_fusion.filt_ref, f32[8,64,128]{2,1,0:T(8,128)S(1)} %get-tuple-element.6.turn_ref, f32[128,128]{1,0:T(8,128)S(1)} %fusion.9.wave_ref, ...), custom_call_target="tpu_custom_call" | custom-call | tf_op jit(solution)/shard_map/pallas_call | solution.py:93
  34.3 20.4 %all_to_all.15 = bf16[64,24,128]{2,1,0:T(8,128)(2,1)S(1)} all-to-all(bf16[64,24,128]{2,1,0:T(8,128)(2,1)S(1)} %shard_map.94), channel_id=1, replica_groups=mesh['seq'=64,'chan'=8] {'seq'}, dimensions={0} | all-to-all | bytes 786432 | tf_op jit(solution)/shard_map/all_to_all | solution.py:140
  54.8 0.0 copy-start.1
  54.8 0.8 slice_convert_fusion
  55.5 0.1 copy-done.1
  55.6 0.4 convolution_bitcast_fusion
  56.0 0.1 reshape.78
  56.1 18.5 %all_to_all.16 = f32[8,1,2048]{2,1,0:T(1,128)S(1)} all-to-all(f32[8,1,2048]{2,1,0:T(1,128)S(1)} %reshape.78), channel_id=1, replica_groups=mesh['seq'=64,'chan'=8] {'chan'}, dimensions={0} | all-to-all | bytes 131072 | tf_op jit(solution)/shard_map/all_to_all | solution.py:145
  74.6 0.5 broadcast.34
  75.1 0.8 %reduce = f32[8,2048]{1,0:T(8,128)S(1)} reduce(f32[8,1,2048]{2,1,0:T(1,128)S(1)} %all_to_all.16, f32[]{:T(128)} %broadcast.34), dimensions={1}, to_apply=%all_to_all.11.reduce_sub_computation | reduce | bytes 131076 | tf_op jit(solution)/shard_map/all_to_all | solution.py:145
  75.9 0.1 reshape.79
  76.0 0.6 reduce_sum.9
  (7 shorter events, 0.1 us)
Async XLA Ops:
  0.6 13.0 %copy-start = (f32[512,64]{0,1:T(8,128)S(1)}, f32[512,64]{0,1:T(8,128)}, u32[]{:S(2)}) copy-start(f32[512,64]{0,1:T(8,128)} %param.9) | copy-start | bytes 393220
  2.4 22.8 %all-to-all-start = ((bf16[64,16,128]{2,1,0:T(8,128)(2,1)}), bf16[64,16,128]{2,1,0:T(8,128)(2,1)S(1)}, u32[]{:S(2)}, u32[]{:S(2)}) async-start(bf16[64,16,128]{2,1,0:T(8,128)(2,1)} %pad_maximum_fusion), calls=%async_computation | async-start | bytes 524288 | tf_op jit(solution)/shard_map/all_to_all | solution.py:134
  13.9 0.7 copy-start.2
  14.6 0.7 copy-start.3
  54.8 0.8 %copy-start.1 = (f32[512,32]{0,1:T(8,128)S(1)}, f32[512,32]{0,1:T(8,128)}, u32[]{:S(2)}) copy-start(f32[512,32]{0,1:T(8,128)} %param.13) | copy-start | bytes 196612
where the time goes:
time: 77 us; the launch traced here: 76.6 us
  blocking collectives  38.9 us (51%)
  starting transfers between devices  10.5 us (14%)
  Pallas kernels  9.12 us (12%)
  waiting for transfers between devices  8.75 us (11%)
  other arithmetic  5.79 us (8%)
  local copies, waits for them, and re-layouts  2.05 us (3%)
  between operations  0.78 us (1%)
    all_to_all x1, blocking collectives, per_device(): home = lax.all_to_all(back, 'seq', split_axis=0, concat_axis=0, tiled=True)  20.4 us
    all_to_all x1, blocking collectives, per_device(): lax.all_to_all(everyone, 'chan', split_axis=0, concat_axis=0, tiled=True)  18.5 us
    all_to_all x1, starting transfers between devices, per_device(): got = lax.all_to_all(sent, 'seq', split_axis=0, concat_axis=0, tiled=True)  10.5 us
    pallas_call x1, Pallas kernels, run_slab(): pl.pallas_call(slab_kernel, out_shape=jax.ShapeDtypeStruct((blocks, 3 * c...  9.12 us
    all_to_all x1, waiting for transfers between devices, per_device(): got = lax.all_to_all(sent, 'seq', split_axis=0, concat_axis=0, tiled=True)  8.75 us
    concatenate x1, other arithmetic, per_device(): jnp.concatenate([inputs.reshape(groups, chans, tok_len), grad_out.reshape...  1.74 us
  transfers between devices with their start and end apart: 1, of which 1 were waited for; matrix products, arithmetic and copies ran while one was open for 3% of the time, Pallas kernels for 0%

commit v1 on v0

--- a/solution.py
+++ b/solution.py
@@ -13,7 +13,7 @@
 highest = lax.Precision.HIGHEST
 
 
-def slab_kernel(got_ref, filt_ref, turn_ref, wave_ref, fall_ref, flip_ref, out_ref, rev_u, rev_f, rows_g, rows_o, mix):
+def slab_kernel(got_ref, filt_ref, turn_ref, wave_ref, fall_ref, flip_ref, out_ref, rev_u, rev_f, rows_g, rows_o, kept):
     blocks = got_ref.shape[0]
     chans = filt_ref.shape[0]
     f32, bf16 = jnp.float32, jnp.bfloat16
@@ -25,19 +25,19 @@
     rows_g[...] = jnp.zeros(rows_g.shape, f32)
     for c in range(chans):
         rev_f[c * pad : c * pad + blocks, :] = filt_ref[c]
+    turned = jnp.dot(got_ref[...].reshape(blocks * 2 * chans, LANES), flip, preferred_element_type=f32)
     for t in range(blocks):
         tile = got_ref[t]
-        turned = jnp.dot(tile, flip, preferred_element_type=f32)
-        rev_u[pl.ds(blocks - 1 - t, chans, stride=pad), :] = turned[:chans]
+        rev_u[pl.ds(blocks - 1 - t, chans, stride=pad), :] = turned[2 * chans * t : 2 * chans * t + chans]
         rows_g[pl.ds(t, chans, stride=gpad), :] = tile.astype(f32)[chans:]
 
     row_id = lax.broadcasted_iota(jnp.int32, (LANES, LANES), 0)
     lane_id = lax.broadcasted_iota(jnp.int32, (LANES, LANES), 1)
-    own = (lane_id <= row_id).astype(f32)
+    own = (lane_id <= row_id).astype(bf16) > 0.5
 
     def rolled(c, d):
         row = jnp.broadcast_to(rows_g[pl.ds(c * gpad + d, 1), :], (LANES, LANES))
-        return pltpu.roll(row, 1, 1, stride=1, stride_axis=0)
+        return pltpu.roll(row, 1, 1, stride=1, stride_axis=0).astype(bf16)
 
     def channel(c, carry):
         acc = [[jnp.zeros((16, LANES), f32) for _ in range(blocks // 16)] for _ in range(2)]
@@ -46,7 +46,7 @@
             pieces = []
             for d in range(d0, d0 + GROUP):
                 after = rolled(c, d + 1)
-                pieces.append(jnp.where(own > 0.5, here, after).astype(bf16))
+                pieces.append(jnp.where(own, here, after))
                 here = after
             hank = jnp.concatenate(pieces, axis=0)
             count = -(-(d0 + GROUP) // 16)
@@ -70,13 +70,13 @@
         grad_h = jnp.concatenate(acc[1], axis=0)
         rows_o[pl.ds(c, blocks, stride=2 * chans), :] = grad_in
         rows_o[pl.ds(c + chans, blocks, stride=2 * chans), :] = grad_h
-        kept = grad_h.astype(bf16).astype(f32) * fall_ref[pl.ds(c, 1), :]
-        spun = jnp.dot(kept, wave_ref[...], precision=highest, preferred_element_type=f32)
-        mix[pl.ds(c, 1), :] = jnp.sum(spun * turn_ref[c], axis=0, keepdims=True)
+        kept[pl.ds(pl.multiple_of(c * blocks, blocks), blocks), :] = grad_h.astype(bf16).astype(f32) * fall_ref[pl.ds(c, 1), :]
         return carry
 
-    lax.fori_loop(0, chans, channel, 0)
-    total = mix[...]
+    lax.fori_loop(0, chans, channel, 0, unroll=True)
+    spun = jnp.dot(kept[...], wave_ref[...], precision=highest, preferred_element_type=f32)
+    spun = spun.reshape(chans, blocks, LANES) * turn_ref[...]
+    total = jnp.sum(spun, axis=1)
     total = total + pltpu.roll(total, LANES // 2, 1)
     high = total.astype(bf16).astype(f32)
     lanes = lax.broadcasted_iota(jnp.int32, total.shape, 1)
@@ -98,7 +98,7 @@
             pltpu.VMEM((chans * 2 * blocks, LANES), f32),
             pltpu.VMEM((chans * (blocks + 8), LANES), f32),
             pltpu.VMEM((2 * chans * blocks, LANES), f32),
-            pltpu.VMEM((chans, LANES), f32),
+            pltpu.VMEM((chans * blocks, LANES), f32),
         ],
         compiler_params=pltpu.CompilerParams(vmem_limit_bytes=32 << 20),
         interpret=interpret,
@@ -120,6 +120,34 @@
     return filt, turn, wave.T, fall
 
 
+def pack_kernel(u_ref, g_ref, out_ref):
+    chans = u_ref.shape[1]
+    out_ref[:, :chans, :] = u_ref[...]
+    out_ref[:, chans:, :] = g_ref[...]
+
+
+def partial_kernel(home_ref, rows_ref, out_ref):
+    groups, rows, lanes = home_ref.shape
+    chans = rows // 3
+    pair = home_ref[:, 2 * chans :, :].astype(jnp.float32).reshape(groups * chans, lanes)
+    sums = jnp.dot(rows_ref[...], pair, precision=highest, preferred_element_type=jnp.float32)
+    sums = sums + pltpu.roll(sums, lanes // 2, 1)
+    half = sums.shape[0] // 2
+    lane_id = lax.broadcasted_iota(jnp.int32, (half, lanes), 1)
+    folded = jnp.where(lane_id < lanes // 2, sums[:half], sums[half:])
+    for part in range(out_ref.shape[0] // half):
+        out_ref[part * half : (part + 1) * half, :] = folded
+
+
+def total_kernel(parts_ref, out_ref):
+    half, lanes = out_ref.shape[0] // 2, parts_ref.shape[1]
+    total = parts_ref[:half]
+    for part in range(1, parts_ref.shape[0] // half):
+        total = total + parts_ref[part * half : (part + 1) * half]
+    out_ref[:half, :] = total[:, : lanes // 2]
+    out_ref[half:, :] = total[:, lanes // 2 :]
+
+
 def per_device(inputs, grad_out, out_weight, decay_rate, frequency, phase_shift, sketch_matrix):
     groups = lax.axis_size("seq")
     parts = lax.axis_size("chan")
@@ -127,9 +155,11 @@
     width_local, tok_len = inputs.shape
     chans = width_local // groups
     order = frequency.shape[0]
+    rank = sketch_matrix.shape[1]
+    f32 = jnp.float32
     first_row = seq_index * chans
-    sent = jnp.concatenate(
-        [inputs.reshape(groups, chans, tok_len), grad_out.reshape(groups, chans, tok_len)], axis=1
+    sent = pl.pallas_call(pack_kernel, out_shape=jax.ShapeDtypeStruct((groups, 2 * chans, tok_len), inputs.dtype))(
+        inputs.reshape(groups, chans, tok_len), grad_out.reshape(groups, chans, tok_len)
     )
     got = lax.all_to_all(sent, "seq", split_axis=0, concat_axis=0, tiled=True)
     rates = lax.dynamic_slice_in_dim(decay_rate, first_row, chans, 0)
@@ -138,11 +168,11 @@
     flip = jnp.eye(LANES, dtype=jnp.bfloat16)[::-1]
     back = run_slab(got, filt, turn, wave, fall, flip)
     home = lax.all_to_all(back, "seq", split_axis=0, concat_axis=0, tiled=True)
-    pair = home[:, 2 * chans :, :].astype(jnp.float32)
-    grad_mix = (pair[:, :, :order] + pair[:, :, order:]).reshape(width_local, order)
-    partial_sum = jnp.dot(sketch_matrix.T, grad_mix, precision=highest, preferred_element_type=jnp.float32)
-    everyone = jnp.broadcast_to(partial_sum[None], (parts, *partial_sum.shape))
-    sketch = jnp.sum(lax.all_to_all(everyone, "chan", split_axis=0, concat_axis=0, tiled=True), axis=0)
+    everyone = pl.pallas_call(partial_kernel, out_shape=jax.ShapeDtypeStruct((parts * rank // 2, LANES), f32))(
+        home, sketch_matrix.T
+    )
+    gathered = lax.all_to_all(everyone, "chan", split_axis=0, concat_axis=0, tiled=True)
+    sketch = pl.pallas_call(total_kernel, out_shape=jax.ShapeDtypeStruct((rank, order), f32))(gathered)
     grad_in = home[:, :chans, :].reshape(width_local, tok_len)
     grad_h = home[:, chans : 2 * chans, :].reshape(width_local, tok_len)
     return (grad_in, grad_h, sketch)

time: 77 us -> 74.5 us (0.968)
  blocking collectives: 38.9 us -> 20.6 us
  starting transfers between devices: 10.5 us -> 20.8 us
  waiting for transfers between devices: 8.75 us -> 16.3 us
  other arithmetic: 5.79 us -> 1.88 us
  Pallas kernels: 9.12 us -> 10.8 us
    all_to_all x1 -> x0, blocking collectives: 18.5 us -> none  [per_device(): lax.all_to_all(everyone, 'chan', split_axis=0, concat_axis=0, tiled=True)]
    all_to_all x0 -> x1, starting transfers between devices: none -> 10.3 us  [per_device(): lax.all_to_all(everyone, 'chan', split_axis=0, concat_axis=0, tiled=True)]
    all_to_all x0 -> x1, waiting for transfers between devices: none -> 7.65 us  [per_device(): lax.all_to_all(everyone, 'chan', split_axis=0, concat_axis=0, tiled=True)]
    pallas_call x0 -> x3, Pallas kernels: none -> 5.29 us  [the longest x1 2.01 us: per_device(): pl.pallas_call(partial_kernel, out_shape=jax.ShapeDtypeStruct((parts * ra...]
    pallas_call x1, Pallas kernels: 9.12 us -> 5.48 us  [run_slab(): pl.pallas_call(slab_kernel, out_shape=jax.ShapeDtypeStruct((blocks, 3 * c...]
    concatenate x1 -> x0, other arithmetic: 1.74 us -> none  [per_device(): jnp.concatenate([inputs.reshape(groups, chans, tok_len), grad_out.reshape...]
    all_to_all x1 -> x0, other arithmetic: 0.8 us -> none  [per_device(): lax.all_to_all(everyone, 'chan', split_axis=0, concat_axis=0, tiled=True)]
  transfers between devices with their start and end apart: 1 -> 2, of which waited for: 1 -> 2; matrix products, arithmetic and copies ran while one was open for 3% -> 4% of each run, Pallas kernels for 0% -> 0%
where the time goes in v1:
time: 74.5 us; the launch traced here: 74.1 us
  starting transfers between devices  20.8 us (28%)
  blocking collectives  20.6 us (28%)
  waiting for transfers between devices  16.3 us (22%)
  Pallas kernels  10.8 us (14%)
  local copies, waits for them, and re-layouts  2.63 us (4%)
  other arithmetic  1.88 us (3%)
  between operations  0.76 us (1%)
    all_to_all x1, blocking collectives, per_device(): home = lax.all_to_all(back, 'seq', split_axis=0, concat_axis=0, tiled=True)  20.6 us
    all_to_all x1, starting transfers between devices, per_device(): got = lax.all_to_all(sent, 'seq', split_axis=0, concat_axis=0, tiled=True)  10.5 us
    all_to_all x1, starting transfers between devices, per_device(): lax.all_to_all(everyone, 'chan', split_axis=0, concat_axis=0, tiled=True)  10.3 us
    all_to_all x1, waiting for transfers between devices, per_device(): got = lax.all_to_all(sent, 'seq', split_axis=0, concat_axis=0, tiled=True)  8.69 us
    all_to_all x1, waiting for transfers between devices, per_device(): lax.all_to_all(everyone, 'chan', split_axis=0, concat_axis=0, tiled=True)  7.65 us
    pallas_call x1, Pallas kernels, run_slab(): pl.pallas_call(slab_kernel, out_shape=jax.ShapeDtypeStruct((blocks, 3 * c...  5.48 us
    pallas_call x1, Pallas kernels, per_device(): pl.pallas_call(partial_kernel, out_shape=jax.ShapeDtypeStruct((parts * ra...  2.01 us
    pallas_call x1, Pallas kernels, per_device(): pl.pallas_call(pack_kernel, out_shape=jax.ShapeDtypeStruct((groups, 2 * c...  1.75 us
  transfers between devices with their start and end apart: 2, of which 2 were waited for; matrix products, arithmetic and copies ran while one was open for 4% of the time, Pallas kernels for 0%

profile of v1, /device:TPU:16, one launch (start us, length us, event | category | flops | bytes accessed | tf_op | source)
XLA Modules:
  0.0 74.1 jit_solution(7930485867024139825)
XLA Ops:
  0.6 0.0 copy-start
  0.6 1.8 %shard_map.94 = bf16[64,16,128]{2,1,0:T(8,128)(2,1)} custom-call(bf16[64,8,128]{2,1,0:T(8,128)(2,1)} %bitcast.17, bf16[64,8,128]{2,1,0:T(8,128)(2,1)} %bitcast.18), custom_call_target="tpu_custom_call" | custom-call | tf_op jit(solution)/shard_map/pallas_call | solution.py:161
  2.4 10.5 %all-to-all-start = ((bf16[64,16,128]{2,1,0:T(8,128)(2,1)}), bf16[64,16,128]{2,1,0:T(8,128)(2,1)S(1)}, u32[]{:S(2)}, u32[]{:S(2)}) async-start(bf16[64,16,128]{2,1,0:T(8,128)(2,1)} %shard_map.94), calls=%async_computation | async-start | bytes 524288 | tf_op jit(solution)/shard_map/all_to_all | solution.py:164
  12.9 0.8 %dynamic-slice_negate_fusion = f32[8]{0:T(128)S(1)} fusion(f32[512]{0:T(512)} %param.10, s32[]{:T(128)S(6)} %select_n.4), kind=kLoop, calls=%fused_computation.20 | loop fusion | flops 8 | bytes 68 | tf_op jit(solution)/shard_map/neg | solution.py:115
  13.7 0.1 multiply_exponential_fusion.fall_ref
  13.8 0.1 multiply_exponential_fusion.1
  13.8 0.1 rev.14
  13.9 0.0 copy-done
  13.9 0.1 constant_dynamic-slice_fusion
  14.0 0.1 copy.16
  14.0 0.1 pad_maximum_fusion.2
  14.1 0.0 copy-start.3
  14.2 0.6 copy-done.3
  14.8 0.0 copy-start.4
  14.8 0.3 multiply_cosine_fusion
  15.1 0.3 copy-done.4
  15.4 0.2 fusion.3
  15.6 0.1 pad_maximum_fusion
  15.8 0.1 pad_maximum_fusion.1
  15.8 0.1 broadcast_multiply_fusion.1
  16.0 0.1 fusion.5.wave_ref
  16.1 0.4 convolution_multiply_fusion.filt_ref
  16.5 8.7 %all-to-all-done.got_ref = bf16[64,16,128]{2,1,0:T(8,128)(2,1)S(1)} async-done(((bf16[64,16,128]{2,1,0:T(8,128)(2,1)}), bf16[64,16,128]{2,1,0:T(8,128)(2,1)S(1)}, u32[]{:S(2)}, u32[]{:S(2)}) %all-to-all-start) | async-done | bytes 262176 | tf_op jit(solution)/shard_map/all_to_all | solution.py:164
  25.2 5.5 %shard_map.95 = bf16[64,24,128]{2,1,0:T(8,128)(2,1)S(1)} custom-call(bf16[64,16,128]{2,1,0:T(8,128)(2,1)S(1)} %all-to-all-done.got_ref, f32[8,64,128]{2,1,0:T(8,128)S(1)} %convolution_multiply_fusion.filt_ref, f32[8,64,128]{2,1,0:T(8,128)S(1)} %get-tuple-element.5.turn_ref, f32[128,128]{1,0:T(8,128)S(1)} %fusion.5.wave_ref, ...), custom_call_target="tpu_custom_call" | custom-call | tf_op jit(solution)/shard_map/pallas_call | solution.py:93
  30.7 20.6 %all_to_all.21.home_ref = bf16[64,24,128]{2,1,0:T(8,128)(2,1)} all-to-all(bf16[64,24,128]{2,1,0:T(8,128)(2,1)S(1)} %shard_map.95), channel_id=1, replica_groups=mesh['seq'=64,'chan'=8] {'seq'}, dimensions={0} | all-to-all | bytes 786432 | tf_op jit(solution)/shard_map/all_to_all | solution.py:170
  51.2 0.0 copy-start.1
  51.2 2.0 %shard_map.96 = f32[128,128]{1,0:T(8,128)} custom-call(bf16[64,24,128]{2,1,0:T(8,128)(2,1)} %all_to_all.21.home_ref, f32[32,512]{1,0:T(8,128)} %bitcast.19), custom_call_target="tpu_custom_call" | custom-call | tf_op jit(solution)/shard_map/pallas_call | solution.py:171
  53.2 10.3 %all-to-all-start.2 = ((f32[8,16,128]{2,1,0:T(8,128)}), f32[8,16,128]{2,1,0:T(8,128)S(1)}, u32[]{:S(2)}, u32[]{:S(2)}) async-start(f32[8,16,128]{2,1,0:T(8,128)} %bitcast.16), calls=%async_computation.2 | async-start | bytes 131072 | tf_op jit(solution)/shard_map/all_to_all | solution.py:174
  63.6 0.0 copy-done.1
  63.6 0.7 slice_bitcast_fusion
  64.3 7.7 %all-to-all-done.2 = f32[8,16,128]{2,1,0:T(8,128)S(1)} async-done(((f32[8,16,128]{2,1,0:T(8,128)}), f32[8,16,128]{2,1,0:T(8,128)S(1)}, u32[]{:S(2)}, u32[]{:S(2)}) %all-to-all-start.2) | async-done | bytes 65568 | tf_op jit(solution)/shard_map/all_to_all | solution.py:174
  71.9 0.0 copy-start.2
  71.9 0.6 copy-done.2
  72.6 1.5 %shard_map.97 = f32[32,64]{1,0:T(8,128)} custom-call(f32[128,128]{1,0:T(8,128)} %bitcast.15), custom_call_target="tpu_custom_call" | custom-call | tf_op jit(solution)/shard_map/pallas_call | solution.py:175
  (6 shorter events, 0.1 us)
Async XLA Ops:
  0.6 13.3 %copy-start = (f32[512,64]{0,1:T(8,128)S(1)}, f32[512,64]{0,1:T(8,128)}, u32[]{:S(2)}) copy-start(f32[512,64]{0,1:T(8,128)} %param.9) | copy-start | bytes 393220
  2.4 22.8 %all-to-all-start = ((bf16[64,16,128]{2,1,0:T(8,128)(2,1)}), bf16[64,16,128]{2,1,0:T(8,128)(2,1)S(1)}, u32[]{:S(2)}, u32[]{:S(2)}) async-start(bf16[64,16,128]{2,1,0:T(8,128)(2,1)} %shard_map.94), calls=%async_computation | async-start | bytes 524288 | tf_op jit(solution)/shard_map/all_to_all | solution.py:164
  14.1 0.7 copy-start.3
  14.8 0.7 copy-start.4
  51.2 12.3 %copy-start.1 = (bf16[64,24,128]{2,1,0:T(8,128)(2,1)S(1)}, bf16[64,24,128]{2,1,0:T(8,128)(2,1)}, u32[]{:S(2)}) copy-start(bf16[64,24,128]{2,1,0:T(8,128)(2,1)} %all_to_all.21.home_ref) | copy-start | bytes 1179652
  53.2 18.7 %all-to-all-start.2 = ((f32[8,16,128]{2,1,0:T(8,128)}), f32[8,16,128]{2,1,0:T(8,128)S(1)}, u32[]{:S(2)}, u32[]{:S(2)}) async-start(f32[8,16,128]{2,1,0:T(8,128)} %bitcast.16), calls=%async_computation.2 | async-start | bytes 131072 | tf_op jit(solution)/shard_map/all_to_all | solution.py:174
  71.9 0.6 copy-start.2

commit v2 on v1

--- a/solution.py
+++ b/solution.py
@@ -9,6 +9,7 @@
 
 LANES = 128
 GROUP = 4
+CHUNKS = 4
 
 highest = lax.Precision.HIGHEST
 
@@ -120,10 +121,27 @@
     return filt, turn, wave.T, fall
 
 
-def pack_kernel(u_ref, g_ref, out_ref):
-    chans = u_ref.shape[1]
-    out_ref[:, :chans, :] = u_ref[...]
-    out_ref[:, chans:, :] = g_ref[...]
+def pack_kernel(u_ref, g_ref, out_ref, both, sems):
+    blocks, chans, _ = u_ref.shape
+    size = blocks // CHUNKS
+    arriving, leaving = [], []
+    for i in range(CHUNKS):
+        span = pl.ds(i * size, size)
+        for s, ref in enumerate((u_ref, g_ref)):
+            copy = pltpu.make_async_copy(
+                ref.at[span], both.at[span, s * chans : (s + 1) * chans, :], sems.at[2 * i + s]
+            )
+            copy.start()
+            arriving.append(copy)
+    for i in range(CHUNKS):
+        span = pl.ds(i * size, size)
+        arriving[2 * i].wait()
+        arriving[2 * i + 1].wait()
+        copy = pltpu.make_async_copy(both.at[span], out_ref.at[span], sems.at[2 * CHUNKS + i])
+        copy.start()
+        leaving.append(copy)
+    for copy in leaving:
+        copy.wait()
 
 
 def partial_kernel(home_ref, rows_ref, out_ref):
@@ -131,21 +149,9 @@
     chans = rows // 3
     pair = home_ref[:, 2 * chans :, :].astype(jnp.float32).reshape(groups * chans, lanes)
     sums = jnp.dot(rows_ref[...], pair, precision=highest, preferred_element_type=jnp.float32)
-    sums = sums + pltpu.roll(sums, lanes // 2, 1)
-    half = sums.shape[0] // 2
-    lane_id = lax.broadcasted_iota(jnp.int32, (half, lanes), 1)
-    folded = jnp.where(lane_id < lanes // 2, sums[:half], sums[half:])
-    for part in range(out_ref.shape[0] // half):
-        out_ref[part * half : (part + 1) * half, :] = folded
-
-
-def total_kernel(parts_ref, out_ref):
-    half, lanes = out_ref.shape[0] // 2, parts_ref.shape[1]
-    total = parts_ref[:half]
-    for part in range(1, parts_ref.shape[0] // half):
-        total = total + parts_ref[part * half : (part + 1) * half]
-    out_ref[:half, :] = total[:, : lanes // 2]
-    out_ref[half:, :] = total[:, lanes // 2 :]
+    folded = sums + pltpu.roll(sums, lanes // 2, 1)
+    for part in range(out_ref.shape[0]):
+        out_ref[part] = folded
 
 
 def per_device(inputs, grad_out, out_weight, decay_rate, frequency, phase_shift, sketch_matrix):
@@ -158,9 +164,16 @@
     rank = sketch_matrix.shape[1]
     f32 = jnp.float32
     first_row = seq_index * chans
-    sent = pl.pallas_call(pack_kernel, out_shape=jax.ShapeDtypeStruct((groups, 2 * chans, tok_len), inputs.dtype))(
-        inputs.reshape(groups, chans, tok_len), grad_out.reshape(groups, chans, tok_len)
-    )
+    sent = pl.pallas_call(
+        pack_kernel,
+        out_shape=jax.ShapeDtypeStruct((groups, 2 * chans, tok_len), inputs.dtype),
+        in_specs=[pl.BlockSpec(memory_space=pl.ANY)] * 2,
+        out_specs=pl.BlockSpec(memory_space=pl.ANY),
+        scratch_shapes=[
+            pltpu.VMEM((groups, 2 * chans, tok_len), inputs.dtype),
+            pltpu.SemaphoreType.DMA((3 * CHUNKS,)),
+        ],
+    )(inputs.reshape(groups, chans, tok_len), grad_out.reshape(groups, chans, tok_len))
     got = lax.all_to_all(sent, "seq", split_axis=0, concat_axis=0, tiled=True)
     rates = lax.dynamic_slice_in_dim(decay_rate, first_row, chans, 0)
     weights = lax.dynamic_slice_in_dim(out_weight, first_row, chans, 0)
@@ -168,11 +181,12 @@
     flip = jnp.eye(LANES, dtype=jnp.bfloat16)[::-1]
     back = run_slab(got, filt, turn, wave, fall, flip)
     home = lax.all_to_all(back, "seq", split_axis=0, concat_axis=0, tiled=True)
-    everyone = pl.pallas_call(partial_kernel, out_shape=jax.ShapeDtypeStruct((parts * rank // 2, LANES), f32))(
-        home, sketch_matrix.T
+    everyone = pl.pallas_call(partial_kernel, out_shape=jax.ShapeDtypeStruct((parts, rank, LANES), f32))(
+        pltpu.with_memory_space_constraint(home, pltpu.VMEM),
+        pltpu.with_memory_space_constraint(sketch_matrix.T, pltpu.VMEM),
     )
     gathered = lax.all_to_all(everyone, "chan", split_axis=0, concat_axis=0, tiled=True)
-    sketch = pl.pallas_call(total_kernel, out_shape=jax.ShapeDtypeStruct((rank, order), f32))(gathered)
+    sketch = jnp.sum(gathered[:, :, :order], axis=0)
     grad_in = home[:, :chans, :].reshape(width_local, tok_len)
     grad_h = home[:, chans : 2 * chans, :].reshape(width_local, tok_len)
     return (grad_in, grad_h, sketch)

time: 74.5 us -> 72.7 us (0.976)
  the two profiles are of different devices: /device:TPU:16 before, /device:TPU:2 now
where the time goes in v2:
time: 72.7 us; the launch traced here: 72.3 us
  starting transfers between devices  21 us (29%)
  blocking collectives  20.3 us (28%)
  waiting for transfers between devices  17.3 us (24%)
  Pallas kernels  8.07 us (11%)
  other arithmetic  2.5 us (3%)
  local copies, waits for them, and re-layouts  2 us (3%)
  between operations  0.78 us (1%)
    all_to_all x1, blocking collectives, per_device(): home = lax.all_to_all(back, 'seq', split_axis=0, concat_axis=0, tiled=True)  20.3 us
    all_to_all x1, starting transfers between devices, per_device(): got = lax.all_to_all(sent, 'seq', split_axis=0, concat_axis=0, tiled=True)  10.7 us
    all_to_all x1, starting transfers between devices, per_device(): lax.all_to_all(everyone, 'chan', split_axis=0, concat_axis=0, tiled=True)  10.3 us
    all_to_all x1, waiting for transfers between devices, per_device(): lax.all_to_all(everyone, 'chan', split_axis=0, concat_axis=0, tiled=True)  8.71 us
    all_to_all x1, waiting for transfers between devices, per_device(): got = lax.all_to_all(sent, 'seq', split_axis=0, concat_axis=0, tiled=True)  8.59 us
    pallas_call x1, Pallas kernels, run_slab(): pl.pallas_call(slab_kernel, out_shape=jax.ShapeDtypeStruct((blocks, 3 * c...  5.48 us
    pallas_call x1, Pallas kernels, per_device(): pl.pallas_call(pack_kernel, out_shape=jax.ShapeDtypeStruct((groups, 2 * c...  1.63 us
  transfers between devices with their start and end apart: 2, of which 2 were waited for; matrix products, arithmetic and copies ran while one was open for 5% of the time, Pallas kernels for 0%

profile of v2, /device:TPU:2, one launch (start us, length us, event | category | flops | bytes accessed | tf_op | source)
XLA Modules:
  0.0 72.3 jit_solution(10217188366374524116)
XLA Ops:
  0.6 0.0 copy-start
  0.6 1.6 %shard_map.94 = bf16[64,16,128]{2,1,0:T(8,128)(2,1)} custom-call(bf16[64,8,128]{2,1,0:T(8,128)(2,1)} %bitcast.14, bf16[64,8,128]{2,1,0:T(8,128)(2,1)} %bitcast.15), custom_call_target="tpu_custom_call" | custom-call | tf_op jit(solution)/shard_map/pallas_call | solution.py:167
  2.3 10.7 %all-to-all-start = ((bf16[64,16,128]{2,1,0:T(8,128)(2,1)}), bf16[64,16,128]{2,1,0:T(8,128)(2,1)S(1)}, u32[]{:S(2)}, u32[]{:S(2)}) async-start(bf16[64,16,128]{2,1,0:T(8,128)(2,1)} %shard_map.94), calls=%async_computation | async-start | bytes 524288 | tf_op jit(solution)/shard_map/all_to_all | solution.py:177
  13.0 0.8 %dynamic-slice_negate_fusion = f32[8]{0:T(128)S(1)} fusion(f32[512]{0:T(512)} %param.10, s32[]{:T(128)S(6)} %select_n.4), kind=kLoop, calls=%fused_computation.21 | loop fusion | flops 8 | bytes 68 | tf_op jit(solution)/shard_map/neg | solution.py:116
  13.8 0.1 multiply_exponential_fusion.fall_ref
  13.8 0.1 multiply_exponential_fusion.1
  13.9 0.1 rev.14
  14.0 0.0 copy-done
  14.0 0.1 constant_dynamic-slice_fusion
  14.1 0.1 copy.16
  14.1 0.1 pad_maximum_fusion.2
  14.2 0.0 copy-start.2
  14.3 0.6 copy-done.2
  14.9 0.0 copy-start.3
  14.9 0.3 multiply_cosine_fusion
  15.2 0.3 copy-done.3
  15.5 0.2 fusion.3
  15.7 0.1 pad_maximum_fusion
  15.8 0.1 pad_maximum_fusion.1
  15.9 0.1 broadcast_multiply_fusion.1
  16.1 0.1 fusion.5.wave_ref
  16.2 0.4 convolution_multiply_fusion.filt_ref
  16.6 8.6 %all-to-all-done.got_ref = bf16[64,16,128]{2,1,0:T(8,128)(2,1)S(1)} async-done(((bf16[64,16,128]{2,1,0:T(8,128)(2,1)}), bf16[64,16,128]{2,1,0:T(8,128)(2,1)S(1)}, u32[]{:S(2)}, u32[]{:S(2)}) %all-to-all-start) | async-done | bytes 262176 | tf_op jit(solution)/shard_map/all_to_all | solution.py:177
  25.2 5.5 %shard_map.95 = bf16[64,24,128]{2,1,0:T(8,128)(2,1)S(1)} custom-call(bf16[64,16,128]{2,1,0:T(8,128)(2,1)S(1)} %all-to-all-done.got_ref, f32[8,64,128]{2,1,0:T(8,128)S(1)} %convolution_multiply_fusion.filt_ref, f32[8,64,128]{2,1,0:T(8,128)S(1)} %get-tuple-element.5.turn_ref, f32[128,128]{1,0:T(8,128)S(1)} %fusion.5.wave_ref, ...), custom_call_target="tpu_custom_call" | custom-call | tf_op jit(solution)/shard_map/pallas_call | solution.py:94
  30.7 0.0 copy-start.1
  30.7 20.3 %all_to_all.15.home_ref = bf16[64,24,128]{2,1,0:T(8,128)(2,1)S(1)} all-to-all(bf16[64,24,128]{2,1,0:T(8,128)(2,1)S(1)} %shard_map.95), channel_id=1, replica_groups=mesh['seq'=64,'chan'=8] {'seq'}, dimensions={0} | all-to-all | bytes 786432 | tf_op jit(solution)/shard_map/all_to_all | solution.py:183
  51.0 0.0 copy-done.1
  51.0 1.0 %shard_map.96 = f32[8,32,128]{2,1,0:T(8,128)} custom-call(bf16[64,24,128]{2,1,0:T(8,128)(2,1)S(1)} %all_to_all.15.home_ref, f32[32,512]{1,0:T(8,128)S(1)} %bitcast.13), custom_call_target="tpu_custom_call" | custom-call | tf_op jit(solution)/shard_map/pallas_call | solution.py:184
  52.0 10.3 %all-to-all-start.2 = ((f32[8,32,128]{2,1,0:T(8,128)}), f32[8,32,128]{2,1,0:T(8,128)S(1)}, u32[]{:S(2)}, u32[]{:S(2)}) async-start(f32[8,32,128]{2,1,0:T(8,128)} %shard_map.96), calls=%async_computation.2 | async-start | bytes 262144 | tf_op jit(solution)/shard_map/all_to_all | solution.py:188
  62.3 0.7 slice_bitcast_fusion
  63.0 8.7 %all-to-all-done.2 = f32[8,32,128]{2,1,0:T(8,128)S(1)} async-done(((f32[8,32,128]{2,1,0:T(8,128)}), f32[8,32,128]{2,1,0:T(8,128)S(1)}, u32[]{:S(2)}, u32[]{:S(2)}) %all-to-all-start.2) | async-done | bytes 131104 | tf_op jit(solution)/shard_map/all_to_all | solution.py:188
  71.7 0.6 slice_reduce_fusion
  (6 shorter events, 0.1 us)
Async XLA Ops:
  0.6 13.4 %copy-start = (f32[512,64]{0,1:T(8,128)S(1)}, f32[512,64]{0,1:T(8,128)}, u32[]{:S(2)}) copy-start(f32[512,64]{0,1:T(8,128)} %param.9) | copy-start | bytes 393220
  2.3 22.9 %all-to-all-start = ((bf16[64,16,128]{2,1,0:T(8,128)(2,1)}), bf16[64,16,128]{2,1,0:T(8,128)(2,1)S(1)}, u32[]{:S(2)}, u32[]{:S(2)}) async-start(bf16[64,16,128]{2,1,0:T(8,128)(2,1)} %shard_map.94), calls=%async_computation | async-start | bytes 524288 | tf_op jit(solution)/shard_map/all_to_all | solution.py:177
  14.2 0.7 copy-start.2
  14.9 0.7 copy-start.3
  30.7 20.3 %copy-start.1 = (f32[512,32]{0,1:T(8,128)S(1)}, f32[512,32]{0,1:T(8,128)}, u32[]{:S(2)}) copy-start(f32[512,32]{0,1:T(8,128)} %param.13) | copy-start | bytes 196612
  52.0 19.7 %all-to-all-start.2 = ((f32[8,32,128]{2,1,0:T(8,128)}), f32[8,32,128]{2,1,0:T(8,128)S(1)}, u32[]{:S(2)}, u32[]{:S(2)}) async-start(f32[8,32,128]{2,1,0:T(8,128)} %shard_map.96), calls=%async_computation.2 | async-start | bytes 262144 | tf_op jit(solution)/shard_map/all_to_all | solution.py:188

commit v3 on v2

v3 whole, which is shorter than its diff:
```python
import math

import jax
import jax.numpy as jnp
from jax import lax
from jax.experimental import pallas as pl
from jax.experimental.pallas import tpu as pltpu
from jax.sharding import PartitionSpec as P

LANES = 128
GROUP = 4
CHUNKS = 4

highest = lax.Precision.HIGHEST


def slab_kernel(got_ref, filt_ref, turn_ref, wave_ref, flip_ref, out_ref, even_u, odd_u, wins_u, rows_g, rows_o, kept):
    blocks = got_ref.shape[0]
    chans = filt_ref.shape[0]
    shifts = filt_ref.shape[2]
    half = LANES // 2
    f32, bf16 = jnp.float32, jnp.bfloat16
    pad = even_u.shape[0] // chans
    gpad = rows_g.shape[0] // chans
    left8 = lax.broadcasted_iota(jnp.int32, (chans, LANES), 1) < half
    for c in range(chans):
        even_u[c * pad + blocks : (c + 1) * pad, :] = jnp.zeros((pad - blocks, LANES), f32)
        odd_u[c * pad + blocks : (c + 1) * pad, :] = jnp.zeros((pad - blocks, LANES), f32)
        rows_g[c * gpad + blocks : (c + 1) * gpad, :] = jnp.zeros((gpad - blocks, LANES), f32)
    turned = jnp.dot(got_ref[...].reshape(blocks * 2 * chans, LANES), flip_ref[...], preferred_element_type=f32)
    last = (jnp.zeros((chans, LANES), f32), jnp.zeros((chans, LANES), f32))
    for t in range(blocks):
        rows = turned[2 * chans * t : 2 * chans * t + chans]
        odd_even, even_odd = rows[:, :LANES], rows[:, LANES:]
        at = blocks - 1 - t
        even_u[pl.ds(at, chans, stride=pad), :] = jnp.where(left8, last[1], odd_even)
        odd_u[pl.ds(at, chans, stride=pad), :] = jnp.where(left8, last[0], even_odd)
        last = (odd_even, even_odd)
        rows_g[pl.ds(t, chans, stride=gpad), :] = got_ref[t].astype(f32)[chans:]

    row_id = lax.broadcasted_iota(jnp.int32, (half, LANES), 0)
    lane_id = lax.broadcasted_iota(jnp.int32, (half, LANES), 1)
    own = (lane_id <= row_id + half).astype(bf16) > 0.5
    left = (lane_id < half).astype(bf16) > 0.5

    for c in range(chans):

        def rolled(d):
            if d >= blocks:
                return jnp.zeros((half, LANES), bf16)
            row = jnp.broadcast_to(rows_g[c * gpad + d : c * gpad + d + 1, :], (half, LANES))
            return pltpu.roll(row, half + 1, 1, stride=1, stride_axis=0).astype(bf16)

        for r in range(shifts):
            wins_u[c, 0, r] = even_u[c * pad + 2 * r : c * pad + 2 * r + blocks, :].astype(bf16)
            wins_u[c, 1, r] = odd_u[c * pad + 2 * r : c * pad + 2 * r + blocks, :].astype(bf16)
        acc = [[[None] * (blocks // 16) for _ in range(2)] for _ in range(2)]
        rolls = [rolled(0), rolled(1)]
        here = jnp.where(own, rolls[0], rolls[1])
        for d0 in range(0, blocks, GROUP):
            hank = ([], [])
            for d in range(d0, d0 + GROUP):
                rolls = [rolls[1], rolled(d + 2)]
                after = jnp.where(own, rolls[0], rolls[1])
                hank[0].append(here)
                hank[1].append(jnp.where(left, after, here))
                here = after
            first = (blocks - 2 - d0) // 16
            count = blocks // 16 - first
            for h in range(2):
                pieces = []
                for wins in (filt_ref, wins_u):
                    pieces.append(
                        jnp.concatenate(
                            [
                                wins[c, h, (blocks - 2 - d) % 16 // 2, 16 * first : blocks, :]
                                for d in range(d0, d0 + GROUP, 2)
                            ],
                            axis=1,
                        )
                    )
                res = jnp.dot(
                    jnp.concatenate(pieces, axis=0), jnp.concatenate(hank[h], axis=0), preferred_element_type=f32
                )
                for s in range(2):
                    for n in range(count):
                        part = res[(s * count + n) * 16 : (s * count + n + 1) * 16]
                        acc[h][s][n] = part if acc[h][s][n] is None else acc[h][s][n] + part
        sums = [
            jnp.concatenate(acc[0][s], axis=0) + pltpu.roll(jnp.concatenate(acc[1][s], axis=0), half, 1)
            for s in range(2)
        ]
        rows_o[pl.ds(c, blocks, stride=2 * chans), :] = sums[0]
        rows_o[pl.ds(c + chans, blocks, stride=2 * chans), :] = sums[1]
        kept[c * blocks : (c + 1) * blocks, :] = sums[1].astype(bf16)
    mixes = []
    for c in range(chans):
        spun = jnp.dot(kept[c * blocks : (c + 1) * blocks, :], wave_ref[c], preferred_element_type=f32)
        spun = (spun[:, :LANES] + spun[:, LANES:]) * turn_ref[c]
        mixes.append(jnp.sum(spun, axis=0, keepdims=True))
    total = jnp.concatenate(mixes, axis=0)
    total = total + pltpu.roll(total, half, 1)
    high = total.astype(bf16).astype(f32)
    pair = jnp.where(left8, high, total - high).astype(bf16)
    for t in range(blocks):
        out_ref[t, : 2 * chans, :] = rows_o[2 * chans * t : 2 * chans * (t + 1), :].astype(bf16)
        out_ref[t, 2 * chans :, :] = pair


def run_slab(got, filt, turn, wave, flip, interpret=False):
    blocks, rows, _ = got.shape
    chans = rows // 2
    f32 = jnp.float32
    return pl.pallas_call(
        slab_kernel,
        out_shape=jax.ShapeDtypeStruct((blocks, 3 * chans, LANES), jnp.bfloat16),
        scratch_shapes=[
            pltpu.VMEM((chans * (blocks + 16), LANES), f32),
            pltpu.VMEM((chans * (blocks + 16), LANES), f32),
            pltpu.VMEM(filt.shape, jnp.bfloat16),
            pltpu.VMEM((chans * (blocks + 8), LANES), f32),
            pltpu.VMEM((2 * chans * blocks, LANES), f32),
            pltpu.VMEM((chans * blocks, LANES), jnp.bfloat16),
        ],
        compiler_params=pltpu.CompilerParams(vmem_limit_bytes=40 << 20),
        interpret=interpret,
    )(got, filt, turn, wave, flip)


def half_windows(filt, blocks):
    after = jnp.pad(filt, ((0, 0), (0, 1), (0, 0)))[:, 1:]
    half = LANES // 2
    even = jnp.concatenate([after[:, :, half:], filt[:, :, half:]], axis=2)
    odd = jnp.concatenate([after[:, :, :half], filt[:, :, :half]], axis=2)
    both = jnp.pad(jnp.stack([even, odd], axis=1), ((0, 0), (0, 0), (0, 16), (0, 0)))
    return jnp.stack([both[:, :, r : r + blocks] for r in range(0, 16, 2)], axis=2).astype(jnp.bfloat16)


def flip_table():
    flip = jnp.eye(LANES, dtype=jnp.bfloat16)[::-1]
    return jnp.concatenate([flip, jnp.roll(flip, LANES // 2, axis=1)], axis=1)


def filter_tables(weights, rates, frequency, phase_shift, blocks):
    hi = (LANES * jnp.arange(blocks)).astype(jnp.float32)
    lo = jnp.arange(LANES).astype(jnp.float32)
    outer = frequency[None, :] * hi[:, None] + phase_shift[None, :]
    inner = frequency[:, None] * lo[None, :]
    turn = jnp.concatenate([jnp.sin(outer), jnp.cos(outer)], axis=1)
    wave = jnp.concatenate([jnp.cos(inner), jnp.sin(inner)], axis=0)
    turn = jnp.exp(-rates[:, None] * hi[None, :])[:, :, None] * turn[None]
    fall = jnp.exp(-rates[:, None] * lo[None, :])
    both = jnp.concatenate([weights, weights], axis=1)
    mixed = jnp.einsum("ckj,jl->ckl", (turn * both[:, None, :])[:, ::-1], wave[:, ::-1], precision=highest)
    filt = mixed * fall[:, None, ::-1]
    spin = fall[:, :, None] * wave.T[None]
    high = lax.reduce_precision(spin, 8, 7)
    spin = jnp.concatenate([high, spin - high], axis=2).astype(jnp.bfloat16)
    return half_windows(filt, blocks), turn, spin


def pack_kernel(u_ref, g_ref, out_ref, both, sems):
    blocks, chans, _ = u_ref.shape
    size = blocks // CHUNKS
    arriving, leaving = [], []
    for i in range(CHUNKS):
        span = pl.ds(i * size, size)
        for s, ref in enumerate((u_ref, g_ref)):
            copy = pltpu.make_async_copy(
                ref.at[span], both.at[span, s * chans : (s + 1) * chans, :], sems.at[2 * i + s]
            )
            copy.start()
            arriving.append(copy)
    for i in range(CHUNKS):
        span = pl.ds(i * size, size)
        arriving[2 * i].wait()
        arriving[2 * i + 1].wait()
        copy = pltpu.make_async_copy(both.at[span], out_ref.at[span], sems.at[2 * CHUNKS + i])
        copy.start()
        leaving.append(copy)
    for copy in leaving:
        copy.wait()


def partial_kernel(home_ref, rows_ref, out_ref):
    groups, rows, lanes = home_ref.shape
    chans = rows // 3
    pair = home_ref[:, 2 * chans :, :].astype(jnp.float32).reshape(groups * chans, lanes)
    sums = jnp.dot(rows_ref[...], pair, precision=highest, preferred_element_type=jnp.float32)
    folded = sums + pltpu.roll(sums, lanes // 2, 1)
    for part in range(out_ref.shape[0]):
        out_ref[part] = folded


def per_device(inputs, grad_out, out_weight, decay_rate, frequency, phase_shift, sketch_matrix):
    groups = lax.axis_size("seq")
    parts = lax.axis_size("chan")
    seq_index = lax.axis_index("seq")
    width_local, tok_len = inputs.shape
    chans = width_local // groups
    order = frequency.shape[0]
    rank = sketch_matrix.shape[1]
    f32 = jnp.float32
    first_row = seq_index * chans
    sent = pl.pallas_call(
        pack_kernel,
        out_shape=jax.ShapeDtypeStruct((groups, 2 * chans, tok_len), inputs.dtype),
        in_specs=[pl.BlockSpec(memory_space=pl.ANY)] * 2,
        out_specs=pl.BlockSpec(memory_space=pl.ANY),
        scratch_shapes=[
            pltpu.VMEM((groups, 2 * chans, tok_len), inputs.dtype),
            pltpu.SemaphoreType.DMA((3 * CHUNKS,)),
        ],
    )(inputs.reshape(groups, chans, tok_len), grad_out.reshape(groups, chans, tok_len))
    got = lax.all_to_all(sent, "seq", split_axis=0, concat_axis=0, tiled=True)
    rates = lax.dynamic_slice_in_dim(decay_rate, first_row, chans, 0)
    weights = lax.dynamic_slice_in_dim(out_weight, first_row, chans, 0)
    filt, turn, wave = filter_tables(weights, rates, frequency, phase_shift, groups)
    flip = flip_table()
    back = run_slab(got, filt, turn, wave, flip)
    home = lax.all_to_all(back, "seq", split_axis=0, concat_axis=0, tiled=True)
    everyone = pl.pallas_call(partial_kernel, out_shape=jax.ShapeDtypeStruct((parts, rank, LANES), f32))(
        pltpu.with_memory_space_constraint(home, pltpu.VMEM),
        pltpu.with_memory_space_constraint(sketch_matrix.T, pltpu.VMEM),
    )
    gathered = lax.all_to_all(everyone, "chan", split_axis=0, concat_axis=0, tiled=True)
    sketch = jnp.sum(gathered[:, :, :order], axis=0)
    grad_in = home[:, :chans, :].reshape(width_local, tok_len)
    grad_h = home[:, chans : 2 * chans, :].reshape(width_local, tok_len)
    return (grad_in, grad_h, sketch)


def solution(mesh):
    placed = (
        P("chan", "seq"),
        P("chan", "seq"),
        P("chan", None),
        P("chan"),
        P(),
        P(),
        P("chan", None),
    )
    return jax.shard_map(
        per_device,
        mesh=mesh,
        in_specs=placed,
        out_specs=(P("chan", "seq"), P("chan", "seq"), P()),
        check_vma=False,
    )
```

time: 72.7 us -> 75.7 us (1.041)
  waiting for transfers between devices: 17.3 us -> 9.01 us
  blocking collectives: 20.3 us -> 24.6 us
  local copies, waits for them, and re-layouts: 2 us -> 6.12 us
  other arithmetic: 2.5 us -> 6.59 us
  Pallas kernels: 8.07 us -> 6.71 us
    all_to_all x1, waiting for transfers between devices: 8.59 us -> 0.3 us  [per_device(): got = lax.all_to_all(sent, 'seq', split_axis=0, concat_axis=0, tiled=True)]
    all_to_all x1, blocking collectives: 20.3 us -> 24.6 us  [per_device(): home = lax.all_to_all(back, 'seq', split_axis=0, concat_axis=0, tiled=True)]
    concatenate x1 -> x2, other arithmetic: 0.08 us -> 1.89 us  [the longest x1 1.01 us: filter_tables(): spin = jnp.concatenate([high, spin - high], axis=2).astype(jnp.bfloat16)]
    slice x0 -> x4, local copies, waits for them, and re-layouts: none -> 1.5 us  [the longest x3 1.35 us: flip_table(): return jnp.concatenate([flip, jnp.roll(flip, LANES // 2, axis=1)], axis=1)]
    pallas_call x1, Pallas kernels: 5.48 us -> 4.12 us  [run_slab(): pl.pallas_call(slab_kernel, out_shape=jax.ShapeDtypeStruct((blocks, 3 * c...]
    another operation x0 -> x3, other arithmetic: none -> 1.1 us
    another operation x0 -> x2, local copies, waits for them, and re-layouts: none -> 1.1 us  [the longest x1 1.08 us: half_windows(): jnp.stack([both[:, :, r:r + blocks] for r in range(0, 16, 2)], axis=2)]
    unnamed x9 -> x13, local copies, waits for them, and re-layouts: 1.05 us -> 1.82 us
  transfers between devices with their start and end apart: 2 -> 2, of which waited for: 2 -> 2; matrix products, arithmetic and copies ran while one was open for 5% -> 16% of each run, Pallas kernels for 0% -> 0%
where the time goes in v3:
time: 75.7 us; the launch traced here: 75.2 us
  blocking collectives  24.6 us (32%)
  starting transfers between devices  21 us (28%)
  waiting for transfers between devices  9.01 us (12%)
  Pallas kernels  6.71 us (9%)
  other arithmetic  6.59 us (9%)
  local copies, waits for them, and re-layouts  6.12 us (8%)
  between operations  0.85 us (1%)
    all_to_all x1, blocking collectives, per_device(): home = lax.all_to_all(back, 'seq', split_axis=0, concat_axis=0, tiled=True)  24.6 us
    all_to_all x1, starting transfers between devices, per_device(): got = lax.all_to_all(sent, 'seq', split_axis=0, concat_axis=0, tiled=True)  10.7 us
    all_to_all x1, starting transfers between devices, per_device(): lax.all_to_all(everyone, 'chan', split_axis=0, concat_axis=0, tiled=True)  10.3 us
    all_to_all x1, waiting for transfers between devices, per_device(): lax.all_to_all(everyone, 'chan', split_axis=0, concat_axis=0, tiled=True)  8.71 us
    pallas_call x1, Pallas kernels, run_slab(): pl.pallas_call(slab_kernel, out_shape=jax.ShapeDtypeStruct((blocks, 3 * c...  4.12 us
    unnamed x13, local copies, waits for them, and re-layouts  1.82 us
    pallas_call x1, Pallas kernels, per_device(): pl.pallas_call(pack_kernel, out_shape=jax.ShapeDtypeStruct((groups, 2 * c...  1.62 us
  transfers between devices with their start and end apart: 2, of which 2 were waited for; matrix products, arithmetic and copies ran while one was open for 16% of the time, Pallas kernels for 0%

profile of v3, /device:TPU:2, one launch (start us, length us, event | category | flops | bytes accessed | tf_op | source)
XLA Modules:
  0.0 75.2 jit_solution(10733339060263118866)
XLA Ops:
  0.6 0.0 copy-start
  0.6 1.6 %shard_map.94 = bf16[64,16,128]{2,1,0:T(8,128)(2,1)} custom-call(bf16[64,8,128]{2,1,0:T(8,128)(2,1)} %bitcast.64, bf16[64,8,128]{2,1,0:T(8,128)(2,1)} %bitcast.65), custom_call_target="tpu_custom_call" | custom-call | tf_op jit(solution)/shard_map/pallas_call | solution.py:205
  2.3 10.7 %all-to-all-start = ((bf16[64,16,128]{2,1,0:T(8,128)(2,1)}), bf16[64,16,128]{2,1,0:T(8,128)(2,1)S(1)}, u32[]{:S(2)}, u32[]{:S(2)}) async-start(bf16[64,16,128]{2,1,0:T(8,128)(2,1)} %shard_map.94), calls=%async_computation | async-start | bytes 524288 | tf_op jit(solution)/shard_map/all_to_all | solution.py:215
  13.0 0.8 %dynamic-slice_negate_fusion = f32[8]{0:T(128)S(1)} fusion(f32[512]{0:T(512)} %param.10, s32[]{:T(128)S(6)} %select_n.4), kind=kLoop, calls=%fused_computation.47 | loop fusion | flops 8 | bytes 68 | tf_op jit(solution)/shard_map/neg | solution.py:151
  13.7 0.0 copy-done
  13.7 0.1 constant_dynamic-slice_fusion
  13.8 0.1 copy.30
  13.9 0.1 pad_maximum_fusion.5
  14.0 0.1 multiply_exponential_fusion.1
  14.0 0.1 multiply_exponential_fusion
  14.1 0.9 %multiply_cosine_fusion = (f32[64,128]{1,0:T(8,128)S(1)}, f32[64,128]{1,0:T(8,128)S(1)}) fusion(f32[128]{0:T(128)S(1)} %iota_convert_fusion, f32[64]{0:T(128)} %param.11), kind=kLoop, calls=%fused_computation.37 | loop fusion | flops 8192 | bytes 66304 | tf_op jit(solution)/shard_map/cos | solution.py:150
  15.0 0.9 %fusion.11 = (f32[64,64]{1,0:T(8,128)S(1)}, f32[64,64]{1,0:T(8,128)S(1)}) fusion(f32[64]{0:T(128)} %param.12, f32[64]{0:T(128)S(1)} %multiply_convert_fusion, f32[64]{0:T(128)} %param.11), kind=kLoop, calls=%fused_computation.41 | loop fusion | flops 8192 | bytes 33536 | tf_op jit(solution)/shard_map/sin | solution.py:149
  15.8 0.1 pad_maximum_fusion.4
  15.9 0.1 broadcast_multiply_fusion.1
  16.1 0.1 rev.14
  16.2 0.1 rev.13
  16.3 0.4 convolution_multiply_fusion
  16.7 0.2 pad_slice_fusion.1
  16.8 0.2 maximum_bitcast_fusion
  17.1 0.1 fusion.13
  17.1 0.6 rev.15
  17.8 0.0 copy-start.2
  17.8 0.1 fusion.7
  17.9 0.1 fusion.6
  18.1 0.1 fusion.5
  18.2 0.1 fusion.3
  18.3 0.2 copy-done.2
  18.5 0.1 copy.29
  18.6 0.9 %reduce-precision_convert_fusion = (bf16[8,128,128]{2,1,0:T(8,128)(2,1)S(1)}, bf16[8,128,128]{2,1,0:T(8,128)(2,1)}) fusion(f32[128,128]{1,0:T(8,128)S(1)} %copy.29, f32[8,128]{1,0:T(8,128)S(1)} %multiply_exponential_fusion), kind=kLoop, calls=%fused_computation.2 | loop fusion | flops 655360 | bytes 593920 | tf_op jit(solution)/shard_map/convert
  19.5 0.6 slice.79
  20.2 0.6 slice.81
  20.8 1.0 %pad_maximum_fusion.1.wave_ref = bf16[8,128,256]{2,1,0:T(8,128)(2,1)S(1)} fusion(bf16[8,128,128]{2,1,0:T(8,128)(2,1)} %get-tuple-element.10, bf16[8,128,128]{2,1,0:T(8,128)(2,1)S(1)} %get-tuple-element.9), kind=kLoop, calls=%fused_computation.6 | loop fusion | flops 1048576 | bytes 1048576 | tf_op jit(solution)/shard_map/concatenate | solution.py:158
  21.8 0.9 %pad_maximum_fusion.3.flip_ref = bf16[128,256]{1,0:T(8,128)(2,1)S(1)} fusion(bf16[128,64]{1,0:T(8,128)(2,1)} %slice.81, bf16[128,64]{1,0:T(8,128)(2,1)} %slice.79, bf16[128,128]{1,0:T(8,128)(2,1)} %rev.15), kind=kLoop, calls=%fused_computation.32 | loop fusion | flops 196608 | bytes 131072 | tf_op jit(solution)/shard_map/concatenate | solution.py:141
  22.7 1.1 %fusion.2 = bf16[8,2,8,64,128]{4,3,2,1,0:T(8,128)(2,1)S(1)} fusion(bf16[8,2,8,64,128]{4,3,2,1,0:T(8,128)(2,1)S(1)} %fusion.3, bf16[8,2,80,128]{3,2,1,0:T(8,128)(2,1)} %copy-done.2), kind=kLoop, calls=%fused_computation.12 | loop fusion | bytes 524288
  23.8 1.1 %fusion.1.filt_ref = bf16[8,2,8,64,128]{4,3,2,1,0:T(8,128)(2,1)S(1)} fusion(bf16[8,2,8,64,128]{4,3,2,1,0:T(8,128)(2,1)S(1)} %fusion.2, bf16[8,2,80,128]{3,2,1,0:T(8,128)(2,1)} %copy-done.2), kind=kLoop, calls=%fused_computation.10 | loop fusion | bytes 524288 | tf_op jit(solution)/shard_map/stack | solution.py:136
  24.9 0.3 all-to-all-done.got_ref
  25.2 0.0 copy-start.1
  25.2 4.1 %shard_map.95 = bf16[64,24,128]{2,1,0:T(8,128)(2,1)S(1)} custom-call(bf16[64,16,128]{2,1,0:T(8,128)(2,1)S(1)} %all-to-all-done.got_ref, bf16[8,2,8,64,128]{4,3,2,1,0:T(8,128)(2,1)S(1)} %fusion.1.filt_ref, f32[8,64,128]{2,1,0:T(8,128)S(1)} %get-tuple-element.13.turn_ref, bf16[8,128,256]{2,1,0:T(8,128)(2,1)S(1)} %pad_maximum_fusion.1.wave_ref, ...), custom_call_target="tpu_custom_call" | custom-call | tf_op jit(solution)/shard_map/pallas_call | solution.py:114
  29.3 24.6 %all_to_all.15.home_ref = bf16[64,24,128]{2,1,0:T(8,128)(2,1)S(1)} all-to-all(bf16[64,24,128]{2,1,0:T(8,128)(2,1)S(1)} %shard_map.95), channel_id=1, replica_groups=mesh['seq'=64,'chan'=8] {'seq'}, dimensions={0} | all-to-all | bytes 786432 | tf_op jit(solution)/shard_map/all_to_all | solution.py:221
  53.9 0.0 copy-done.1
  53.9 1.0 %shard_map.96 = f32[8,32,128]{2,1,0:T(8,128)} custom-call(bf16[64,24,128]{2,1,0:T(8,128)(2,1)S(1)} %all_to_all.15.home_ref, f32[32,512]{1,0:T(8,128)S(1)} %bitcast.63), custom_call_target="tpu_custom_call" | custom-call | tf_op jit(solution)/shard_map/pallas_call | solution.py:222
  54.8 10.3 %all-to-all-start.2 = ((f32[8,32,128]{2,1,0:T(8,128)}), f32[8,32,128]{2,1,0:T(8,128)S(1)}, u32[]{:S(2)}, u32[]{:S(2)}) async-start(f32[8,32,128]{2,1,0:T(8,128)} %shard_map.96), calls=%async_computation.2 | async-start | bytes 262144 | tf_op jit(solution)/shard_map/all_to_all | solution.py:226
  65.2 0.7 slice_bitcast_fusion.7
  65.9 8.7 %all-to-all-done.2 = f32[8,32,128]{2,1,0:T(8,128)S(1)} async-done(((f32[8,32,128]{2,1,0:T(8,128)}), f32[8,32,128]{2,1,0:T(8,128)S(1)}, u32[]{:S(2)}, u32[]{:S(2)}) %all-to-all-start.2) | async-done | bytes 131104 | tf_op jit(solution)/shard_map/all_to_all | solution.py:226
  74.6 0.6 slice_reduce_fusion
  (9 shorter events, 0.2 us)
Async XLA Ops:
  0.6 13.1 %copy-start = (f32[512,64]{0,1:T(8,128)S(1)}, f32[512,64]{0,1:T(8,128)}, u32[]{:S(2)}) copy-start(f32[512,64]{0,1:T(8,128)} %param.9) | copy-start | bytes 393220
  2.3 22.9 %all-to-all-start = ((bf16[64,16,128]{2,1,0:T(8,128)(2,1)}), bf16[64,16,128]{2,1,0:T(8,128)(2,1)S(1)}, u32[]{:S(2)}, u32[]{:S(2)}) async-start(bf16[64,16,128]{2,1,0:T(8,128)(2,1)} %shard_map.94), calls=%async_computation | async-start | bytes 524288 | tf_op jit(solution)/shard_map/all_to_all | solution.py:215
  17.8 0.7 copy-start.2
  25.2 28.7 %copy-start.1 = (f32[512,32]{0,1:T(8,128)S(1)}, f32[512,32]{0,1:T(8,128)}, u32[]{:S(2)}) copy-start(f32[512,32]{0,1:T(8,128)} %param.13) | copy-start | bytes 196612
  54.8 19.7 %all-to-all-start.2 = ((f32[8,32,128]{2,1,0:T(8,128)}), f32[8,32,128]{2,1,0:T(8,128)S(1)}, u32[]{:S(2)}, u32[]{:S(2)}) async-start(f32[8,32,128]{2,1,0:T(8,128)} %shard_map.96), calls=%async_computation.2 | async-start | bytes 262144 | tf_op jit(solution)/shard_map/all_to_all | solution.py:226

commit v4 on v3

--- a/solution.py
+++ b/solution.py
@@ -127,36 +127,75 @@
     )(got, filt, turn, wave, flip)
 
 
-def half_windows(filt, blocks):
-    after = jnp.pad(filt, ((0, 0), (0, 1), (0, 0)))[:, 1:]
+def filter_kernel(
+    turn_ref, wave_ref, rise_ref, fall_ref, both_ref, filt_ref, mix_ref, spin_ref, flip_ref, rows, even, odd
+):
+    blocks = turn_ref.shape[1]
+    chans = both_ref.shape[1]
+    shifts = filt_ref.shape[2]
+    pad = rows.shape[0] // chans
     half = LANES // 2
-    even = jnp.concatenate([after[:, :, half:], filt[:, :, half:]], axis=2)
-    odd = jnp.concatenate([after[:, :, :half], filt[:, :, :half]], axis=2)
-    both = jnp.pad(jnp.stack([even, odd], axis=1), ((0, 0), (0, 0), (0, 16), (0, 0)))
-    return jnp.stack([both[:, :, r : r + blocks] for r in range(0, 16, 2)], axis=2).astype(jnp.bfloat16)
-
-
-def flip_table():
-    flip = jnp.eye(LANES, dtype=jnp.bfloat16)[::-1]
-    return jnp.concatenate([flip, jnp.roll(flip, LANES // 2, axis=1)], axis=1)
-
-
-def filter_tables(weights, rates, frequency, phase_shift, blocks):
-    hi = (LANES * jnp.arange(blocks)).astype(jnp.float32)
-    lo = jnp.arange(LANES).astype(jnp.float32)
-    outer = frequency[None, :] * hi[:, None] + phase_shift[None, :]
-    inner = frequency[:, None] * lo[None, :]
-    turn = jnp.concatenate([jnp.sin(outer), jnp.cos(outer)], axis=1)
-    wave = jnp.concatenate([jnp.cos(inner), jnp.sin(inner)], axis=0)
-    turn = jnp.exp(-rates[:, None] * hi[None, :])[:, :, None] * turn[None]
-    fall = jnp.exp(-rates[:, None] * lo[None, :])
-    both = jnp.concatenate([weights, weights], axis=1)
-    mixed = jnp.einsum("ckj,jl->ckl", (turn * both[:, None, :])[:, ::-1], wave[:, ::-1], precision=highest)
-    filt = mixed * fall[:, None, ::-1]
-    spin = fall[:, :, None] * wave.T[None]
-    high = lax.reduce_precision(spin, 8, 7)
-    spin = jnp.concatenate([high, spin - high], axis=2).astype(jnp.bfloat16)
-    return half_windows(filt, blocks), turn, spin
+    f32, bf16 = jnp.float32, jnp.bfloat16
+    left = lax.broadcasted_iota(jnp.int32, (blocks, LANES), 1) < half
+    mixed = []
+    for c in range(chans):
+        mix_ref[c] = turn_ref[0] * rise_ref[0, :, c : c + 1]
+        mixed.append(turn_ref[1] * rise_ref[1, :, c : c + 1] * both_ref[0, c : c + 1, :])
+        spin = wave_ref[0] * fall_ref[:, c : c + 1]
+        high = spin.astype(bf16)
+        spin_ref[c, :, :LANES] = high
+        spin_ref[c, :, LANES:] = (spin - high.astype(f32)).astype(bf16)
+    filt = jnp.dot(jnp.concatenate(mixed, axis=0), wave_ref[1], precision=highest, preferred_element_type=f32)
+    blank = jnp.zeros((pad - blocks, LANES), f32)
+    for c in range(chans):
+        own = filt[c * blocks : (c + 1) * blocks] * both_ref[1, c : c + 1, :]
+        rows[c * pad : c * pad + blocks, :] = own
+        rows[c * pad + blocks : (c + 1) * pad, :] = blank
+        after = rows[c * pad + 1 : c * pad + 1 + blocks, :]
+        even[c * pad : c * pad + blocks, :] = jnp.where(left, pltpu.roll(after, half, 1), own)
+        odd[c * pad : c * pad + blocks, :] = jnp.where(left, after, pltpu.roll(own, half, 1))
+        even[c * pad + blocks : (c + 1) * pad, :] = blank
+        odd[c * pad + blocks : (c + 1) * pad, :] = blank
+        for r in range(shifts):
+            filt_ref[c, 0, r] = even[c * pad + 2 * r : c * pad + 2 * r + blocks, :].astype(bf16)
+            filt_ref[c, 1, r] = odd[c * pad + 2 * r : c * pad + 2 * r + blocks, :].astype(bf16)
+    ends = lax.broadcasted_iota(jnp.int32, (LANES, 2 * LANES), 0) + lax.broadcasted_iota(
+        jnp.int32, (LANES, 2 * LANES), 1
+    )
+    lane = lax.broadcasted_iota(jnp.int32, (LANES, 2 * LANES), 1)
+    turned = (ends == LANES + half - 1) | (ends == 2 * LANES + half - 1)
+    flip_ref[...] = jnp.where(lane < LANES, jnp.where(ends == LANES - 1, 1.0, 0.0), jnp.where(turned, 1.0, 0.0)).astype(bf16)
+
+
+def filter_tables(weights, rates, frequency, phase_shift, blocks, interpret=False):
+    f32, bf16 = jnp.float32, jnp.bfloat16
+    chans = rates.shape[0]
+    hi = (LANES * jnp.arange(blocks)).astype(f32)
+    lo = jnp.arange(LANES).astype(f32)
+    twice = jnp.concatenate([frequency, frequency])
+    quarter = jnp.arange(2 * frequency.shape[0]) < frequency.shape[0]
+    hi = jnp.stack([hi, hi[::-1]])
+    outer = twice[None, None, :] * hi[:, :, None] + jnp.concatenate([phase_shift, phase_shift])[None, None, :]
+    turn = jnp.where(quarter, jnp.sin(outer), jnp.cos(outer))
+    inner = twice[None, :] * lo[:, None]
+    plain = jnp.where(quarter, jnp.cos(inner), jnp.sin(inner))
+    inner = twice[:, None] * lo[None, ::-1]
+    wave = jnp.stack([plain, jnp.where(quarter[:, None], jnp.cos(inner), jnp.sin(inner))])
+    rise = jnp.exp(-rates[None, None, :] * hi[:, :, None])
+    fall = jnp.exp(-rates[None, :] * lo[:, None])
+    both = jnp.stack([jnp.concatenate([weights, weights], axis=1), jnp.exp(-rates[:, None] * lo[None, ::-1])])
+    return pl.pallas_call(
+        filter_kernel,
+        out_shape=(
+            jax.ShapeDtypeStruct((chans, 2, 8, blocks, LANES), bf16),
+            jax.ShapeDtypeStruct((chans, blocks, LANES), f32),
+            jax.ShapeDtypeStruct((chans, LANES, 2 * LANES), bf16),
+            jax.ShapeDtypeStruct((LANES, 2 * LANES), bf16),
+        ),
+        scratch_shapes=[pltpu.VMEM((chans * (blocks + 16), LANES), f32)] * 3,
+        compiler_params=pltpu.CompilerParams(vmem_limit_bytes=32 << 20),
+        interpret=interpret,
+    )(turn, wave, rise, fall, both)
 
 
 def pack_kernel(u_ref, g_ref, out_ref, both, sems):
@@ -215,8 +254,7 @@
     got = lax.all_to_all(sent, "seq", split_axis=0, concat_axis=0, tiled=True)
     rates = lax.dynamic_slice_in_dim(decay_rate, first_row, chans, 0)
     weights = lax.dynamic_slice_in_dim(out_weight, first_row, chans, 0)
-    filt, turn, wave = filter_tables(weights, rates, frequency, phase_shift, groups)
-    flip = flip_table()
+    filt, turn, wave, flip = filter_tables(weights, rates, frequency, phase_shift, groups)
     back = run_slab(got, filt, turn, wave, flip)
     home = lax.all_to_all(back, "seq", split_axis=0, concat_axis=0, tiled=True)
     everyone = pl.pallas_call(partial_kernel, out_shape=jax.ShapeDtypeStruct((parts, rank, LANES), f32))(

time: 75.7 us -> 71.2 us (0.941)
  waiting for transfers between devices: 9.01 us -> 16.9 us
  local copies, waits for them, and re-layouts: 6.12 us -> 1.06 us
  blocking collectives: 24.6 us -> 20.2 us
  other arithmetic: 6.59 us -> 3.42 us
  Pallas kernels: 6.71 us -> 7.57 us
    all_to_all x1, waiting for transfers between devices: 0.3 us -> 8.16 us  [per_device(): got = lax.all_to_all(sent, 'seq', split_axis=0, concat_axis=0, tiled=True)]
    all_to_all x1, blocking collectives: 24.6 us -> 20.2 us  [per_device(): home = lax.all_to_all(back, 'seq', split_axis=0, concat_axis=0, tiled=True)]
    unnamed x13 -> x5, local copies, waits for them, and re-layouts: 1.82 us -> 0.07 us
    slice x4 -> x0, local copies, waits for them, and re-layouts: 1.5 us -> none  [the longest x3 1.35 us: flip_table(): return jnp.concatenate([flip, jnp.roll(flip, LANES // 2, axis=1)], axis=1)]
    concatenate x4 -> x1, other arithmetic: 2.04 us -> 0.82 us  [filter_tables(): twice = jnp.concatenate([frequency, frequency])]
    another operation x2 -> x0, local copies, waits for them, and re-layouts: 1.1 us -> none  [the longest x1 1.08 us: half_windows(): jnp.stack([both[:, :, r:r + blocks] for r in range(0, 16, 2)], axis=2)]
    another operation x3 -> x4, other arithmetic: 1.1 us -> 0.1 us  [the longest x2 0.08 us: filter_tables(): jnp.stack([jnp.concatenate([weights, weights], axis=1), jnp.exp(-rates[:,...]
    sin x1 -> x0, other arithmetic: 0.87 us -> none  [filter_tables(): turn = jnp.concatenate([jnp.sin(outer), jnp.cos(outer)], axis=1)]
  transfers between devices with their start and end apart: 2 -> 2, of which waited for: 2 -> 2; matrix products, arithmetic and copies ran while one was open for 16% -> 5% of each run, Pallas kernels for 0% -> 1%
where the time goes in v4:
time: 71.2 us; the launch traced here: 70.9 us
  starting transfers between devices  21 us (29%)
  blocking collectives  20.2 us (28%)
  waiting for transfers between devices  16.9 us (24%)
  Pallas kernels  7.57 us (11%)
  other arithmetic  3.42 us (5%)
  local copies, waits for them, and re-layouts  1.06 us (1%)
  between operations  0.76 us (1%)
    all_to_all x1, blocking collectives, per_device(): home = lax.all_to_all(back, 'seq', split_axis=0, concat_axis=0, tiled=True)  20.2 us
    all_to_all x1, starting transfers between devices, per_device(): got = lax.all_to_all(sent, 'seq', split_axis=0, concat_axis=0, tiled=True)  10.7 us
    all_to_all x1, starting transfers between devices, per_device(): lax.all_to_all(everyone, 'chan', split_axis=0, concat_axis=0, tiled=True)  10.3 us
    all_to_all x1, waiting for transfers between devices, per_device(): lax.all_to_all(everyone, 'chan', split_axis=0, concat_axis=0, tiled=True)  8.71 us
    all_to_all x1, waiting for transfers between devices, per_device(): got = lax.all_to_all(sent, 'seq', split_axis=0, concat_axis=0, tiled=True)  8.16 us
    pallas_call x1, Pallas kernels, run_slab(): pl.pallas_call(slab_kernel, out_shape=jax.ShapeDtypeStruct((blocks, 3 * c...  4.13 us
    pallas_call x1, Pallas kernels, per_device(): pl.pallas_call(pack_kernel, out_shape=jax.ShapeDtypeStruct((groups, 2 * c...  1.64 us
  transfers between devices with their start and end apart: 2, of which 2 were waited for; matrix products, arithmetic and copies ran while one was open for 5% of the time, Pallas kernels for 1%

profile of v4, /device:TPU:2, one launch (start us, length us, event | category | flops | bytes accessed | tf_op | source)
XLA Modules:
  0.0 70.9 jit_solution(4137678013767399442)
XLA Ops:
  0.6 0.0 copy-start
  0.6 1.6 %shard_map.94 = bf16[64,16,128]{2,1,0:T(8,128)(2,1)} custom-call(bf16[64,8,128]{2,1,0:T(8,128)(2,1)} %bitcast.11, bf16[64,8,128]{2,1,0:T(8,128)(2,1)} %bitcast.12), custom_call_target="tpu_custom_call" | custom-call | tf_op jit(solution)/shard_map/pallas_call | solution.py:244
  2.3 10.7 %all-to-all-start = ((bf16[64,16,128]{2,1,0:T(8,128)(2,1)}), bf16[64,16,128]{2,1,0:T(8,128)(2,1)S(1)}, u32[]{:S(2)}, u32[]{:S(2)}) async-start(bf16[64,16,128]{2,1,0:T(8,128)(2,1)} %shard_map.94), calls=%async_computation | async-start | bytes 524288 | tf_op jit(solution)/shard_map/all_to_all | solution.py:254
  13.0 0.1 rev.8
  13.1 0.1 rev.7
  13.2 0.8 %dynamic-slice_negate_fusion = f32[8]{0:T(128)S(1)} fusion(f32[512]{0:T(512)} %param.10, s32[]{:T(128)S(6)} %select_n.33), kind=kLoop, calls=%fused_computation.19 | loop fusion | flops 8 | bytes 68 | tf_op jit(solution)/shard_map/neg | solution.py:184
  14.0 0.1 multiply_exponential_fusion.fall_ref
  14.1 0.1 multiply_exponential_fusion.2
  14.1 0.0 copy-done
  14.1 0.1 constant_dynamic-slice_fusion
  14.2 0.1 copy.13
  14.3 0.1 maximum_bitcast_fusion
  14.4 0.8 %pad_maximum_fusion.3 = (f32[128]{0:T(128)S(1)}, f32[128]{0:T(128)S(1)}) fusion(f32[64]{0:T(128)} %param.11, f32[64]{0:T(128)} %param.12), kind=kLoop, calls=%fused_computation.17 | loop fusion | flops 256 | bytes 1536 | tf_op jit(solution)/shard_map/concatenate | solution.py:175
  15.2 0.5 fusion
  15.8 0.1 multiply_exponential_fusion.1.rise_ref
  15.9 0.3 cosine_select_fusion.turn_ref
  16.2 0.8 %shard_map.95 = (bf16[8,2,8,64,128]{4,3,2,1,0:T(8,128)(2,1)S(1)}, f32[8,64,128]{2,1,0:T(8,128)S(1)}, bf16[8,128,256]{2,1,0:T(8,128)(2,1)S(1)}, bf16[128,256]{1,0:T(8,128)(2,1)S(1)}) custom-call(f32[2,64,128]{2,1,0:T(8,128)S(1)} %cosine_select_fusion.turn_ref, f32[2,128,128]{2,1,0:T(8,128)S(1)} %pad_maximum_fusion.wave_ref, ...), custom_call_target="tpu_custom_call" | custom-call | tf_op jit(solution)/shard_map/pallas_call | solution.py:187
  17.0 8.2 %all-to-all-done.got_ref = bf16[64,16,128]{2,1,0:T(8,128)(2,1)S(1)} async-done(((bf16[64,16,128]{2,1,0:T(8,128)(2,1)}), bf16[64,16,128]{2,1,0:T(8,128)(2,1)S(1)}, u32[]{:S(2)}, u32[]{:S(2)}) %all-to-all-start) | async-done | bytes 262176 | tf_op jit(solution)/shard_map/all_to_all | solution.py:254
  25.2 0.0 copy-start.1
  25.2 4.1 %shard_map.96 = bf16[64,24,128]{2,1,0:T(8,128)(2,1)S(1)} custom-call(bf16[64,16,128]{2,1,0:T(8,128)(2,1)S(1)} %all-to-all-done.got_ref, bf16[8,2,8,64,128]{4,3,2,1,0:T(8,128)(2,1)S(1)} %get-tuple-element.7.filt_ref, f32[8,64,128]{2,1,0:T(8,128)S(1)} %get-tuple-element.8.turn_ref, bf16[8,128,256]{2,1,0:T(8,128)(2,1)S(1)} %get-tuple-element.9.wave_ref, ...), custom_call_target="tpu_custom_call" | custom-call | tf_op jit(solution)/shard_map/pallas_call | solution.py:114
  29.3 20.2 %all_to_all.15.home_ref = bf16[64,24,128]{2,1,0:T(8,128)(2,1)S(1)} all-to-all(bf16[64,24,128]{2,1,0:T(8,128)(2,1)S(1)} %shard_map.96), channel_id=1, replica_groups=mesh['seq'=64,'chan'=8] {'seq'}, dimensions={0} | all-to-all | bytes 786432 | tf_op jit(solution)/shard_map/all_to_all | solution.py:259
  49.5 0.0 copy-done.1
  49.5 1.0 %shard_map.97 = f32[8,32,128]{2,1,0:T(8,128)} custom-call(bf16[64,24,128]{2,1,0:T(8,128)(2,1)S(1)} %all_to_all.15.home_ref, f32[32,512]{1,0:T(8,128)S(1)} %bitcast.10), custom_call_target="tpu_custom_call" | custom-call | tf_op jit(solution)/shard_map/pallas_call | solution.py:260
  50.5 10.3 %all-to-all-start.2 = ((f32[8,32,128]{2,1,0:T(8,128)}), f32[8,32,128]{2,1,0:T(8,128)S(1)}, u32[]{:S(2)}, u32[]{:S(2)}) async-start(f32[8,32,128]{2,1,0:T(8,128)} %shard_map.97), calls=%async_computation.2 | async-start | bytes 262144 | tf_op jit(solution)/shard_map/all_to_all | solution.py:264
  60.8 0.7 %slice_bitcast_fusion = (bf16[512,128]{1,0:T(8,128)(2,1)}, bf16[512,128]{1,0:T(8,128)(2,1)}) fusion(bf16[64,24,128]{2,1,0:T(8,128)(2,1)S(1)} %all_to_all.15.home_ref), kind=kLoop, calls=%fused_computation.1 | loop fusion | bytes 524288 | tf_op jit(solution)/shard_map/reshape | solution.py:267
  61.5 8.7 %all-to-all-done.2 = f32[8,32,128]{2,1,0:T(8,128)S(1)} async-done(((f32[8,32,128]{2,1,0:T(8,128)}), f32[8,32,128]{2,1,0:T(8,128)S(1)}, u32[]{:S(2)}, u32[]{:S(2)}) %all-to-all-start.2) | async-done | bytes 131104 | tf_op jit(solution)/shard_map/all_to_all | solution.py:264
  70.2 0.6 slice_reduce_fusion
  (7 shorter events, 0.0 us)
Async XLA Ops:
  0.6 13.5 %copy-start = (f32[512,64]{0,1:T(8,128)S(1)}, f32[512,64]{0,1:T(8,128)}, u32[]{:S(2)}) copy-start(f32[512,64]{0,1:T(8,128)} %param.9) | copy-start | bytes 393220
  2.3 22.9 %all-to-all-start = ((bf16[64,16,128]{2,1,0:T(8,128)(2,1)}), bf16[64,16,128]{2,1,0:T(8,128)(2,1)S(1)}, u32[]{:S(2)}, u32[]{:S(2)}) async-start(bf16[64,16,128]{2,1,0:T(8,128)(2,1)} %shard_map.94), calls=%async_computation | async-start | bytes 524288 | tf_op jit(solution)/shard_map/all_to_all | solution.py:254
  25.2 24.3 %copy-start.1 = (f32[512,32]{0,1:T(8,128)S(1)}, f32[512,32]{0,1:T(8,128)}, u32[]{:S(2)}) copy-start(f32[512,32]{0,1:T(8,128)} %param.13) | copy-start | bytes 196612
  50.5 19.7 %all-to-all-start.2 = ((f32[8,32,128]{2,1,0:T(8,128)}), f32[8,32,128]{2,1,0:T(8,128)S(1)}, u32[]{:S(2)}, u32[]{:S(2)}) async-start(f32[8,32,128]{2,1,0:T(8,128)} %shard_map.97), calls=%async_computation.2 | async-start | bytes 262144 | tf_op jit(solution)/shard_map/all_to_all | solution.py:264

commit v5 on v4

--- a/solution.py
+++ b/solution.py
@@ -221,14 +221,22 @@
         copy.wait()
 
 
-def partial_kernel(home_ref, rows_ref, out_ref):
+def unpack_kernel(home_ref, rows_ref, in_ref, h_ref, part_ref, sems):
     groups, rows, lanes = home_ref.shape
     chans = rows // 3
+    copies = [
+        pltpu.make_async_copy(home_ref.at[:, s * chans : (s + 1) * chans, :], ref, sems.at[s])
+        for s, ref in enumerate((in_ref, h_ref))
+    ]
+    for copy in copies:
+        copy.start()
     pair = home_ref[:, 2 * chans :, :].astype(jnp.float32).reshape(groups * chans, lanes)
     sums = jnp.dot(rows_ref[...], pair, precision=highest, preferred_element_type=jnp.float32)
     folded = sums + pltpu.roll(sums, lanes // 2, 1)
-    for part in range(out_ref.shape[0]):
-        out_ref[part] = folded
+    for part in range(part_ref.shape[0]):
+        part_ref[part] = folded
+    for copy in copies:
+        copy.wait()
 
 
 def per_device(inputs, grad_out, out_weight, decay_rate, frequency, phase_shift, sketch_matrix):
@@ -257,15 +265,23 @@
     filt, turn, wave, flip = filter_tables(weights, rates, frequency, phase_shift, groups)
     back = run_slab(got, filt, turn, wave, flip)
     home = lax.all_to_all(back, "seq", split_axis=0, concat_axis=0, tiled=True)
-    everyone = pl.pallas_call(partial_kernel, out_shape=jax.ShapeDtypeStruct((parts, rank, LANES), f32))(
+    gradient = jax.ShapeDtypeStruct((groups, chans, tok_len), home.dtype)
+    grad_in, grad_h, everyone = pl.pallas_call(
+        unpack_kernel,
+        out_shape=(gradient, gradient, pltpu.VMEM((parts, rank, LANES), f32)),
+        out_specs=(
+            pl.BlockSpec(memory_space=pl.ANY),
+            pl.BlockSpec(memory_space=pl.ANY),
+            pl.BlockSpec(memory_space=pltpu.VMEM),
+        ),
+        scratch_shapes=[pltpu.SemaphoreType.DMA((2,))],
+    )(
         pltpu.with_memory_space_constraint(home, pltpu.VMEM),
         pltpu.with_memory_space_constraint(sketch_matrix.T, pltpu.VMEM),
     )
     gathered = lax.all_to_all(everyone, "chan", split_axis=0, concat_axis=0, tiled=True)
     sketch = jnp.sum(gathered[:, :, :order], axis=0)
-    grad_in = home[:, :chans, :].reshape(width_local, tok_len)
-    grad_h = home[:, chans : 2 * chans, :].reshape(width_local, tok_len)
-    return (grad_in, grad_h, sketch)
+    return (grad_in.reshape(width_local, tok_len), grad_h.reshape(width_local, tok_len), sketch)
 
 
 def solution(mesh):

time: 71.2 us -> 70.8 us (level)
  blocking collectives: 20.2 us -> 39.7 us
  starting transfers between devices: 21 us -> 10.7 us
  waiting for transfers between devices: 16.9 us -> 8.17 us
  local copies, waits for them, and re-layouts: 1.06 us -> 0.34 us
    all_to_all x0 -> x1, blocking collectives: none -> 19.5 us  [per_device(): lax.all_to_all(everyone, 'chan', split_axis=0, concat_axis=0, tiled=True)]
    all_to_all x1 -> x0, starting transfers between devices: 10.3 us -> none  [per_device(): lax.all_to_all(everyone, 'chan', split_axis=0, concat_axis=0, tiled=True)]
    all_to_all x1 -> x0, waiting for transfers between devices: 8.71 us -> none  [per_device(): lax.all_to_all(everyone, 'chan', split_axis=0, concat_axis=0, tiled=True)]
    reshape x1 -> x0, local copies, waits for them, and re-layouts: 0.72 us -> none  [per_device(): grad_h = home[:, chans:2 * chans, :].reshape(width_local, tok_len)]
  transfers between devices with their start and end apart: 2 -> 1, of which waited for: 2 -> 1; matrix products, arithmetic and copies ran while one was open for 5% -> 4% of each run, Pallas kernels for 1% -> 1%
where the time goes in v5:
time: 70.8 us; the launch traced here: 70.5 us
  blocking collectives  39.7 us (56%)
  starting transfers between devices  10.7 us (15%)
  waiting for transfers between devices  8.17 us (12%)
  Pallas kernels  7.39 us (10%)
  other arithmetic  3.42 us (5%)
  between operations  0.76 us (1%)
    all_to_all x1, blocking collectives, per_device(): home = lax.all_to_all(back, 'seq', split_axis=0, concat_axis=0, tiled=True)  20.2 us
    all_to_all x1, blocking collectives, per_device(): lax.all_to_all(everyone, 'chan', split_axis=0, concat_axis=0, tiled=True)  19.5 us
    all_to_all x1, starting transfers between devices, per_device(): got = lax.all_to_all(sent, 'seq', split_axis=0, concat_axis=0, tiled=True)  10.7 us
    all_to_all x1, waiting for transfers between devices, per_device(): got = lax.all_to_all(sent, 'seq', split_axis=0, concat_axis=0, tiled=True)  8.17 us
    pallas_call x1, Pallas kernels, run_slab(): pl.pallas_call(slab_kernel, out_shape=jax.ShapeDtypeStruct((blocks, 3 * c...  4.12 us
    pallas_call x1, Pallas kernels, per_device(): pl.pallas_call(pack_kernel, out_shape=jax.ShapeDtypeStruct((groups, 2 * c...  1.64 us
  transfers between devices with their start and end apart: 1, of which 1 were waited for; matrix products, arithmetic and copies ran while one was open for 4% of the time, Pallas kernels for 1%

profile of v5, /device:TPU:2, one launch (start us, length us, event | category | flops | bytes accessed | tf_op | source)
XLA Modules:
  0.0 70.5 jit_solution(14012534231368148582)
XLA Ops:
  0.6 0.0 copy-start
  0.6 1.6 %shard_map.94 = bf16[64,16,128]{2,1,0:T(8,128)(2,1)} custom-call(bf16[64,8,128]{2,1,0:T(8,128)(2,1)} %bitcast.9, bf16[64,8,128]{2,1,0:T(8,128)(2,1)} %bitcast.10), custom_call_target="tpu_custom_call" | custom-call | tf_op jit(solution)/shard_map/pallas_call | solution.py:252
  2.3 10.7 %all-to-all-start = ((bf16[64,16,128]{2,1,0:T(8,128)(2,1)}), bf16[64,16,128]{2,1,0:T(8,128)(2,1)S(1)}, u32[]{:S(2)}, u32[]{:S(2)}) async-start(bf16[64,16,128]{2,1,0:T(8,128)(2,1)} %shard_map.94), calls=%async_computation | async-start | bytes 524288 | tf_op jit(solution)/shard_map/all_to_all | solution.py:262
  13.0 0.1 rev.8
  13.1 0.1 rev.7
  13.2 0.8 %dynamic-slice_negate_fusion = f32[8]{0:T(128)S(1)} fusion(f32[512]{0:T(512)} %param.10, s32[]{:T(128)S(6)} %select_n.33), kind=kLoop, calls=%fused_computation.17 | loop fusion | flops 8 | bytes 68 | tf_op jit(solution)/shard_map/neg | solution.py:184
  14.0 0.1 multiply_exponential_fusion.fall_ref
  14.1 0.1 multiply_exponential_fusion.2
  14.1 0.0 copy-done
  14.1 0.1 constant_dynamic-slice_fusion
  14.2 0.1 copy.13
  14.3 0.1 maximum_bitcast_fusion
  14.4 0.8 %pad_maximum_fusion.3 = (f32[128]{0:T(128)S(1)}, f32[128]{0:T(128)S(1)}) fusion(f32[64]{0:T(128)} %param.11, f32[64]{0:T(128)} %param.12), kind=kLoop, calls=%fused_computation.15 | loop fusion | flops 256 | bytes 1536 | tf_op jit(solution)/shard_map/concatenate | solution.py:175
  15.2 0.5 fusion
  15.8 0.1 multiply_exponential_fusion.1.rise_ref
  15.9 0.3 cosine_select_fusion.turn_ref
  16.2 0.8 %shard_map.95 = (bf16[8,2,8,64,128]{4,3,2,1,0:T(8,128)(2,1)S(1)}, f32[8,64,128]{2,1,0:T(8,128)S(1)}, bf16[8,128,256]{2,1,0:T(8,128)(2,1)S(1)}, bf16[128,256]{1,0:T(8,128)(2,1)S(1)}) custom-call(f32[2,64,128]{2,1,0:T(8,128)S(1)} %cosine_select_fusion.turn_ref, f32[2,128,128]{2,1,0:T(8,128)S(1)} %pad_maximum_fusion.wave_ref, ...), custom_call_target="tpu_custom_call" | custom-call | tf_op jit(solution)/shard_map/pallas_call | solution.py:187
  17.0 8.2 %all-to-all-done.got_ref = bf16[64,16,128]{2,1,0:T(8,128)(2,1)S(1)} async-done(((bf16[64,16,128]{2,1,0:T(8,128)(2,1)}), bf16[64,16,128]{2,1,0:T(8,128)(2,1)S(1)}, u32[]{:S(2)}, u32[]{:S(2)}) %all-to-all-start) | async-done | bytes 262176 | tf_op jit(solution)/shard_map/all_to_all | solution.py:262
  25.2 0.0 copy-start.1
  25.2 4.1 %shard_map.96 = bf16[64,24,128]{2,1,0:T(8,128)(2,1)S(1)} custom-call(bf16[64,16,128]{2,1,0:T(8,128)(2,1)S(1)} %all-to-all-done.got_ref, bf16[8,2,8,64,128]{4,3,2,1,0:T(8,128)(2,1)S(1)} %get-tuple-element.10.filt_ref, f32[8,64,128]{2,1,0:T(8,128)S(1)} %get-tuple-element.11.turn_ref, bf16[8,128,256]{2,1,0:T(8,128)(2,1)S(1)} %get-tuple-element.12.wave_ref, ...), custom_call_target="tpu_custom_call" | custom-call | tf_op jit(solution)/shard_map/pallas_call | solution.py:114
  29.3 20.2 %all_to_all.15.home_ref = bf16[64,24,128]{2,1,0:T(8,128)(2,1)S(1)} all-to-all(bf16[64,24,128]{2,1,0:T(8,128)(2,1)S(1)} %shard_map.96), channel_id=1, replica_groups=mesh['seq'=64,'chan'=8] {'seq'}, dimensions={0} | all-to-all | bytes 786432 | tf_op jit(solution)/shard_map/all_to_all | solution.py:267
  49.5 0.0 copy-done.1
  49.5 0.8 %shard_map.97 = (bf16[64,8,128]{2,1,0:T(8,128)(2,1)}, bf16[64,8,128]{2,1,0:T(8,128)(2,1)}, f32[8,32,128]{2,1,0:T(8,128)S(1)}) custom-call(bf16[64,24,128]{2,1,0:T(8,128)(2,1)S(1)} %all_to_all.15.home_ref, f32[32,512]{1,0:T(8,128)S(1)} %bitcast.8), custom_call_target="tpu_custom_call" | custom-call | tf_op jit(solution)/shard_map/pallas_call | solution.py:269
  50.3 19.5 %all_to_all.16 = f32[8,32,128]{2,1,0:T(8,128)S(1)} all-to-all(f32[8,32,128]{2,1,0:T(8,128)S(1)} %get-tuple-element.16), channel_id=1, replica_groups=mesh['seq'=64,'chan'=8] {'chan'}, dimensions={0} | all-to-all | bytes 262144 | tf_op jit(solution)/shard_map/all_to_all | solution.py:282
  69.9 0.6 slice_reduce_fusion
  (7 shorter events, 0.0 us)
Async XLA Ops:
  0.6 13.5 %copy-start = (f32[512,64]{0,1:T(8,128)S(1)}, f32[512,64]{0,1:T(8,128)}, u32[]{:S(2)}) copy-start(f32[512,64]{0,1:T(8,128)} %param.9) | copy-start | bytes 393220
  2.3 22.9 %all-to-all-start = ((bf16[64,16,128]{2,1,0:T(8,128)(2,1)}), bf16[64,16,128]{2,1,0:T(8,128)(2,1)S(1)}, u32[]{:S(2)}, u32[]{:S(2)}) async-start(bf16[64,16,128]{2,1,0:T(8,128)(2,1)} %shard_map.94), calls=%async_computation | async-start | bytes 524288 | tf_op jit(solution)/shard_map/all_to_all | solution.py:262
  25.2 24.3 %copy-start.1 = (f32[512,32]{0,1:T(8,128)S(1)}, f32[512,32]{0,1:T(8,128)}, u32[]{:S(2)}) copy-start(f32[512,32]{0,1:T(8,128)} %param.13) | copy-start | bytes 196612

commit v6 on v5

--- a/solution.py
+++ b/solution.py
@@ -27,10 +27,11 @@
         even_u[c * pad + blocks : (c + 1) * pad, :] = jnp.zeros((pad - blocks, LANES), f32)
         odd_u[c * pad + blocks : (c + 1) * pad, :] = jnp.zeros((pad - blocks, LANES), f32)
         rows_g[c * gpad + blocks : (c + 1) * gpad, :] = jnp.zeros((gpad - blocks, LANES), f32)
-    turned = jnp.dot(got_ref[...].reshape(blocks * 2 * chans, LANES), flip_ref[...], preferred_element_type=f32)
+    both = got_ref[:, :chans, :].astype(f32).reshape(blocks * chans, LANES).astype(bf16)
+    turned = jnp.dot(both, flip_ref[...], preferred_element_type=f32)
     last = (jnp.zeros((chans, LANES), f32), jnp.zeros((chans, LANES), f32))
     for t in range(blocks):
-        rows = turned[2 * chans * t : 2 * chans * t + chans]
+        rows = turned[chans * t : chans * (t + 1)]
         odd_even, even_odd = rows[:, :LANES], rows[:, LANES:]
         at = blocks - 1 - t
         even_u[pl.ds(at, chans, stride=pad), :] = jnp.where(left8, last[1], odd_even)
@@ -230,13 +231,21 @@
     ]
     for copy in copies:
         copy.start()
-    pair = home_ref[:, 2 * chans :, :].astype(jnp.float32).reshape(groups * chans, lanes)
-    sums = jnp.dot(rows_ref[...], pair, precision=highest, preferred_element_type=jnp.float32)
+    pair = home_ref[:, 2 * chans :, :].astype(jnp.float32).reshape(groups * chans, lanes).astype(jnp.bfloat16)
+    sums = jnp.dot(rows_ref[...], pair, preferred_element_type=jnp.float32)
+    rank = part_ref.shape[1]
+    sums = sums[:rank] + (sums[rank : 2 * rank] + sums[2 * rank :])
     folded = sums + pltpu.roll(sums, lanes // 2, 1)
     for part in range(part_ref.shape[0]):
         part_ref[part] = folded
     for copy in copies:
         copy.wait()
+
+
+def three_parts(values):
+    high = lax.reduce_precision(values, 8, 7)
+    middle = lax.reduce_precision(values - high, 8, 7)
+    return jnp.concatenate([high, middle, values - high - middle], axis=0).astype(jnp.bfloat16)
 
 
 def per_device(inputs, grad_out, out_weight, decay_rate, frequency, phase_shift, sketch_matrix):
@@ -277,7 +286,7 @@
         scratch_shapes=[pltpu.SemaphoreType.DMA((2,))],
     )(
         pltpu.with_memory_space_constraint(home, pltpu.VMEM),
-        pltpu.with_memory_space_constraint(sketch_matrix.T, pltpu.VMEM),
+        pltpu.with_memory_space_constraint(three_parts(sketch_matrix.T), pltpu.VMEM),
     )
     gathered = lax.all_to_all(everyone, "chan", split_axis=0, concat_axis=0, tiled=True)
     sketch = jnp.sum(gathered[:, :, :order], axis=0)

time: 70.8 us -> 71.7 us (1.013)
  blocking collectives: 39.7 us -> 19.5 us
  waiting for transfers between devices: 8.17 us -> 22.9 us
  starting transfers between devices: 10.7 us -> 16.3 us
    all_to_all x1 -> x0, blocking collectives: 20.2 us -> none  [per_device(): home = lax.all_to_all(back, 'seq', split_axis=0, concat_axis=0, tiled=True)]
    all_to_all x0 -> x1, waiting for transfers between devices: none -> 14.7 us  [per_device(): home = lax.all_to_all(back, 'seq', split_axis=0, concat_axis=0, tiled=True)]
    all_to_all x0 -> x1, starting transfers between devices: none -> 5.65 us  [per_device(): home = lax.all_to_all(back, 'seq', split_axis=0, concat_axis=0, tiled=True)]
    pallas_call x1, Pallas kernels: 4.12 us -> 4.85 us  [run_slab(): pl.pallas_call(slab_kernel, out_shape=jax.ShapeDtypeStruct((blocks, 3 * c...]
  transfers between devices with their start and end apart: 1 -> 2, of which waited for: 1 -> 2; matrix products, arithmetic and copies ran while one was open for 4% -> 4% of each run, Pallas kernels for 1% -> 1%
where the time goes in v6:
time: 71.7 us; the launch traced here: 71.3 us
  waiting for transfers between devices  22.9 us (32%)
  blocking collectives  19.5 us (27%)
  starting transfers between devices  16.3 us (23%)
  Pallas kernels  8.04 us (11%)
  other arithmetic  3.44 us (5%)
  between operations  0.79 us (1%)
    all_to_all x1, blocking collectives, per_device(): lax.all_to_all(everyone, 'chan', split_axis=0, concat_axis=0, tiled=True)  19.5 us
    all_to_all x1, waiting for transfers between devices, per_device(): home = lax.all_to_all(back, 'seq', split_axis=0, concat_axis=0, tiled=True)  14.7 us
    all_to_all x1, starting transfers between devices, per_device(): got = lax.all_to_all(sent, 'seq', split_axis=0, concat_axis=0, tiled=True)  10.7 us
    all_to_all x1, waiting for transfers between devices, per_device(): got = lax.all_to_all(sent, 'seq', split_axis=0, concat_axis=0, tiled=True)  8.17 us
    all_to_all x1, starting transfers between devices, per_device(): home = lax.all_to_all(back, 'seq', split_axis=0, concat_axis=0, tiled=True)  5.65 us
    pallas_call x1, Pallas kernels, run_slab(): pl.pallas_call(slab_kernel, out_shape=jax.ShapeDtypeStruct((blocks, 3 * c...  4.85 us
    pallas_call x1, Pallas kernels, per_device(): pl.pallas_call(pack_kernel, out_shape=jax.ShapeDtypeStruct((groups, 2 * c...  1.63 us
  transfers between devices with their start and end apart: 2, of which 2 were waited for; matrix products, arithmetic and copies ran while one was open for 4% of the time, Pallas kernels for 1%

profile of v6, /device:TPU:2, one launch (start us, length us, event | category | flops | bytes accessed | tf_op | source)
XLA Modules:
  0.0 71.3 jit_solution(8273199963989856416)
XLA Ops:
  0.6 0.0 copy-start
  0.6 1.6 %shard_map.94 = bf16[64,16,128]{2,1,0:T(8,128)(2,1)} custom-call(bf16[64,8,128]{2,1,0:T(8,128)(2,1)} %bitcast.14, bf16[64,8,128]{2,1,0:T(8,128)(2,1)} %bitcast.15), custom_call_target="tpu_custom_call" | custom-call | tf_op jit(solution)/shard_map/pallas_call | solution.py:261
  2.3 10.7 %all-to-all-start = ((bf16[64,16,128]{2,1,0:T(8,128)(2,1)}), bf16[64,16,128]{2,1,0:T(8,128)(2,1)S(1)}, u32[]{:S(2)}, u32[]{:S(2)}) async-start(bf16[64,16,128]{2,1,0:T(8,128)(2,1)} %shard_map.94), calls=%async_computation | async-start | bytes 524288 | tf_op jit(solution)/shard_map/all_to_all | solution.py:271
  13.0 0.1 rev.8
  13.1 0.8 %dynamic-slice_negate_fusion = f32[8]{0:T(128)S(1)} fusion(f32[512]{0:T(512)} %param.10, s32[]{:T(128)S(6)} %select_n.33), kind=kLoop, calls=%fused_computation.23 | loop fusion | flops 8 | bytes 68 | tf_op jit(solution)/shard_map/neg | solution.py:185
  13.9 0.1 multiply_exponential_fusion.fall_ref
  14.0 0.1 multiply_exponential_fusion.2
  14.0 0.0 copy-done
  14.0 0.1 constant_dynamic-slice_fusion
  14.1 0.1 copy.13
  14.2 0.1 maximum_bitcast_fusion
  14.3 0.1 rev.7
  14.4 0.8 %pad_maximum_fusion.4 = (f32[128]{0:T(128)S(1)}, f32[128]{0:T(128)S(1)}) fusion(f32[64]{0:T(128)} %param.11, f32[64]{0:T(128)} %param.12), kind=kLoop, calls=%fused_computation.21 | loop fusion | flops 256 | bytes 1536 | tf_op jit(solution)/shard_map/concatenate | solution.py:176
  15.2 0.5 fusion
  15.8 0.1 multiply_exponential_fusion.1.rise_ref
  15.9 0.3 cosine_select_fusion.turn_ref
  16.2 0.8 %shard_map.95 = (bf16[8,2,8,64,128]{4,3,2,1,0:T(8,128)(2,1)S(1)}, f32[8,64,128]{2,1,0:T(8,128)S(1)}, bf16[8,128,256]{2,1,0:T(8,128)(2,1)S(1)}, bf16[128,256]{1,0:T(8,128)(2,1)S(1)}) custom-call(f32[2,64,128]{2,1,0:T(8,128)S(1)} %cosine_select_fusion.turn_ref, f32[2,128,128]{2,1,0:T(8,128)S(1)} %pad_maximum_fusion.wave_ref, ...), custom_call_target="tpu_custom_call" | custom-call | tf_op jit(solution)/shard_map/pallas_call | solution.py:188
  17.0 8.2 %all-to-all-done.got_ref = bf16[64,16,128]{2,1,0:T(8,128)(2,1)S(1)} async-done(((bf16[64,16,128]{2,1,0:T(8,128)(2,1)}), bf16[64,16,128]{2,1,0:T(8,128)(2,1)S(1)}, u32[]{:S(2)}, u32[]{:S(2)}) %all-to-all-start) | async-done | bytes 262176 | tf_op jit(solution)/shard_map/all_to_all | solution.py:271
  25.2 0.0 copy-start.1
  25.2 4.8 %shard_map.96 = bf16[64,24,128]{2,1,0:T(8,128)(2,1)} custom-call(bf16[64,16,128]{2,1,0:T(8,128)(2,1)S(1)} %all-to-all-done.got_ref, bf16[8,2,8,64,128]{4,3,2,1,0:T(8,128)(2,1)S(1)} %get-tuple-element.10.filt_ref, f32[8,64,128]{2,1,0:T(8,128)S(1)} %get-tuple-element.11.turn_ref, bf16[8,128,256]{2,1,0:T(8,128)(2,1)S(1)} %get-tuple-element.12.wave_ref, ...), custom_call_target="tpu_custom_call" | custom-call | tf_op jit(solution)/shard_map/pallas_call | solution.py:115
  30.0 5.7 %all-to-all-start.1 = ((bf16[64,24,128]{2,1,0:T(8,128)(2,1)}), bf16[64,24,128]{2,1,0:T(8,128)(2,1)S(1)}, u32[]{:S(2)}, u32[]{:S(2)}) async-start(bf16[64,24,128]{2,1,0:T(8,128)(2,1)} %shard_map.96), calls=%async_computation.1 | async-start | bytes 786432 | tf_op jit(solution)/shard_map/all_to_all | solution.py:276
  35.7 0.0 copy-done.1
  35.7 14.7 %all-to-all-done.1.home_ref = bf16[64,24,128]{2,1,0:T(8,128)(2,1)S(1)} async-done(((bf16[64,24,128]{2,1,0:T(8,128)(2,1)}), bf16[64,24,128]{2,1,0:T(8,128)(2,1)S(1)}, u32[]{:S(2)}, u32[]{:S(2)}) %all-to-all-start.1) | async-done | bytes 393248 | tf_op jit(solution)/shard_map/all_to_all | solution.py:276
  50.4 0.7 %shard_map.97 = (bf16[64,8,128]{2,1,0:T(8,128)(2,1)}, bf16[64,8,128]{2,1,0:T(8,128)(2,1)}, f32[8,32,128]{2,1,0:T(8,128)S(1)}) custom-call(bf16[64,24,128]{2,1,0:T(8,128)(2,1)S(1)} %all-to-all-done.1.home_ref, bf16[96,512]{1,0:T(8,128)(2,1)S(1)} %pad_maximum_fusion.1.rows_ref), custom_call_target="tpu_custom_call" | custom-call | tf_op jit(solution)/shard_map/pallas_call | solution.py:278
  51.2 19.5 %all_to_all.15 = f32[8,32,128]{2,1,0:T(8,128)S(1)} all-to-all(f32[8,32,128]{2,1,0:T(8,128)S(1)} %get-tuple-element.16), channel_id=1, replica_groups=mesh['seq'=64,'chan'=8] {'chan'}, dimensions={0} | all-to-all | bytes 262144 | tf_op jit(solution)/shard_map/all_to_all | solution.py:291
  70.7 0.6 slice_reduce_fusion
  (9 shorter events, 0.1 us)
Async XLA Ops:
  0.6 13.4 %copy-start = (f32[512,64]{0,1:T(8,128)S(1)}, f32[512,64]{0,1:T(8,128)}, u32[]{:S(2)}) copy-start(f32[512,64]{0,1:T(8,128)} %param.9) | copy-start | bytes 393220
  2.3 22.9 %all-to-all-start = ((bf16[64,16,128]{2,1,0:T(8,128)(2,1)}), bf16[64,16,128]{2,1,0:T(8,128)(2,1)S(1)}, u32[]{:S(2)}, u32[]{:S(2)}) async-start(bf16[64,16,128]{2,1,0:T(8,128)(2,1)} %shard_map.94), calls=%async_computation | async-start | bytes 524288 | tf_op jit(solution)/shard_map/all_to_all | solution.py:271
  25.2 10.5 %copy-start.1 = (f32[512,32]{0,1:T(8,128)S(1)}, f32[512,32]{0,1:T(8,128)}, u32[]{:S(2)}) copy-start(f32[512,32]{0,1:T(8,128)} %param.13) | copy-start | bytes 196612
  30.0 20.4 %all-to-all-start.1 = ((bf16[64,24,128]{2,1,0:T(8,128)(2,1)}), bf16[64,24,128]{2,1,0:T(8,128)(2,1)S(1)}, u32[]{:S(2)}, u32[]{:S(2)}) async-start(bf16[64,24,128]{2,1,0:T(8,128)(2,1)} %shard_map.96), calls=%async_computation.1 | async-start | bytes 786432 | tf_op jit(solution)/shard_map/all_to_all | solution.py:276

commit v7 on v6

--- a/solution.py
+++ b/solution.py
@@ -129,7 +129,8 @@
 
 
 def filter_kernel(
-    turn_ref, wave_ref, rise_ref, fall_ref, both_ref, filt_ref, mix_ref, spin_ref, flip_ref, rows, even, odd
+    turn_ref, wave_ref, rise_ref, fall_ref, both_ref, sketch_ref,
+    filt_ref, mix_ref, spin_ref, flip_ref, parts_ref, rows, even, odd,
 ):
     blocks = turn_ref.shape[1]
     chans = both_ref.shape[1]
@@ -138,6 +139,12 @@
     half = LANES // 2
     f32, bf16 = jnp.float32, jnp.bfloat16
     left = lax.broadcasted_iota(jnp.int32, (blocks, LANES), 1) < half
+    rest = sketch_ref[...]
+    rank = rest.shape[0]
+    for part in range(3):
+        piece = rest.astype(bf16)
+        parts_ref[part * rank : (part + 1) * rank, :] = piece
+        rest = rest - piece.astype(f32)
     mixed = []
     for c in range(chans):
         mix_ref[c] = turn_ref[0] * rise_ref[0, :, c : c + 1]
@@ -168,7 +175,7 @@
     flip_ref[...] = jnp.where(lane < LANES, jnp.where(ends == LANES - 1, 1.0, 0.0), jnp.where(turned, 1.0, 0.0)).astype(bf16)
 
 
-def filter_tables(weights, rates, frequency, phase_shift, blocks, interpret=False):
+def filter_tables(weights, rates, frequency, phase_shift, sketch_rows, blocks, interpret=False):
     f32, bf16 = jnp.float32, jnp.bfloat16
     chans = rates.shape[0]
     hi = (LANES * jnp.arange(blocks)).astype(f32)
@@ -192,11 +199,12 @@
             jax.ShapeDtypeStruct((chans, blocks, LANES), f32),
             jax.ShapeDtypeStruct((chans, LANES, 2 * LANES), bf16),
             jax.ShapeDtypeStruct((LANES, 2 * LANES), bf16),
+            jax.ShapeDtypeStruct((3 * sketch_rows.shape[0], sketch_rows.shape[1]), bf16),
         ),
         scratch_shapes=[pltpu.VMEM((chans * (blocks + 16), LANES), f32)] * 3,
         compiler_params=pltpu.CompilerParams(vmem_limit_bytes=32 << 20),
         interpret=interpret,
-    )(turn, wave, rise, fall, both)
+    )(turn, wave, rise, fall, both, sketch_rows)
 
 
 def pack_kernel(u_ref, g_ref, out_ref, both, sems):
@@ -240,12 +248,6 @@
         part_ref[part] = folded
     for copy in copies:
         copy.wait()
-
-
-def three_parts(values):
-    high = lax.reduce_precision(values, 8, 7)
-    middle = lax.reduce_precision(values - high, 8, 7)
-    return jnp.concatenate([high, middle, values - high - middle], axis=0).astype(jnp.bfloat16)
 
 
 def per_device(inputs, grad_out, out_weight, decay_rate, frequency, phase_shift, sketch_matrix):
@@ -271,7 +273,9 @@
     got = lax.all_to_all(sent, "seq", split_axis=0, concat_axis=0, tiled=True)
     rates = lax.dynamic_slice_in_dim(decay_rate, first_row, chans, 0)
     weights = lax.dynamic_slice_in_dim(out_weight, first_row, chans, 0)
-    filt, turn, wave, flip = filter_tables(weights, rates, frequency, phase_shift, groups)
+    filt, turn, wave, flip, sketch_parts = filter_tables(
+        weights, rates, frequency, phase_shift, sketch_matrix.T, groups
+    )
     back = run_slab(got, filt, turn, wave, flip)
     home = lax.all_to_all(back, "seq", split_axis=0, concat_axis=0, tiled=True)
     gradient = jax.ShapeDtypeStruct((groups, chans, tok_len), home.dtype)
@@ -286,7 +290,7 @@
         scratch_shapes=[pltpu.SemaphoreType.DMA((2,))],
     )(
         pltpu.with_memory_space_constraint(home, pltpu.VMEM),
-        pltpu.with_memory_space_constraint(three_parts(sketch_matrix.T), pltpu.VMEM),
+        pltpu.with_memory_space_constraint(sketch_parts, pltpu.VMEM),
     )
     gathered = lax.all_to_all(everyone, "chan", split_axis=0, concat_axis=0, tiled=True)
     sketch = jnp.sum(gathered[:, :, :order], axis=0)

time: 71.7 us -> 70.7 us (0.986)
  blocking collectives: 19.5 us -> 39.7 us
  waiting for transfers between devices: 22.9 us -> 7.33 us
  starting transfers between devices: 16.3 us -> 10.7 us
  local copies, waits for them, and re-layouts: 0.34 us -> 1.18 us
  Pallas kernels: 8.04 us -> 7.3 us
    all_to_all x0 -> x1, blocking collectives: none -> 20.2 us  [per_device(): home = lax.all_to_all(back, 'seq', split_axis=0, concat_axis=0, tiled=True)]
    all_to_all x1 -> x0, waiting for transfers between devices: 14.7 us -> none  [per_device(): home = lax.all_to_all(back, 'seq', split_axis=0, concat_axis=0, tiled=True)]
    all_to_all x1 -> x0, starting transfers between devices: 5.65 us -> none  [per_device(): home = lax.all_to_all(back, 'seq', split_axis=0, concat_axis=0, tiled=True)]
    all_to_all x1, waiting for transfers between devices: 8.17 us -> 7.33 us  [per_device(): got = lax.all_to_all(sent, 'seq', split_axis=0, concat_axis=0, tiled=True)]
    unnamed x5, local copies, waits for them, and re-layouts: 0.07 us -> 0.91 us
    pallas_call x1, Pallas kernels: 4.85 us -> 4.1 us  [run_slab(): pl.pallas_call(slab_kernel, out_shape=jax.ShapeDtypeStruct((blocks, 3 * c...]
  transfers between devices with their start and end apart: 2 -> 1, of which waited for: 2 -> 1; matrix products, arithmetic and copies ran while one was open for 4% -> 4% of each run, Pallas kernels for 1% -> 1%
where the time goes in v7:
time: 70.7 us; the launch traced here: 70.4 us
  blocking collectives  39.7 us (56%)
  starting transfers between devices  10.7 us (15%)
  waiting for transfers between devices  7.33 us (10%)
  Pallas kernels  7.3 us (10%)
  other arithmetic  3.42 us (5%)
  local copies, waits for them, and re-layouts  1.18 us (2%)
  between operations  0.77 us (1%)
    all_to_all x1, blocking collectives, per_device(): home = lax.all_to_all(back, 'seq', split_axis=0, concat_axis=0, tiled=True)  20.2 us
    all_to_all x1, blocking collectives, per_device(): lax.all_to_all(everyone, 'chan', split_axis=0, concat_axis=0, tiled=True)  19.5 us
    all_to_all x1, starting transfers between devices, per_device(): got = lax.all_to_all(sent, 'seq', split_axis=0, concat_axis=0, tiled=True)  10.7 us
    all_to_all x1, waiting for transfers between devices, per_device(): got = lax.all_to_all(sent, 'seq', split_axis=0, concat_axis=0, tiled=True)  7.33 us
    pallas_call x1, Pallas kernels, run_slab(): pl.pallas_call(slab_kernel, out_shape=jax.ShapeDtypeStruct((blocks, 3 * c...  4.1 us
    pallas_call x1, Pallas kernels, per_device(): pl.pallas_call(pack_kernel, out_shape=jax.ShapeDtypeStruct((groups, 2 * c...  1.64 us
  transfers between devices with their start and end apart: 1, of which 1 were waited for; matrix products, arithmetic and copies ran while one was open for 4% of the time, Pallas kernels for 1%

profile of v7, /device:TPU:2, one launch (start us, length us, event | category | flops | bytes accessed | tf_op | source)
XLA Modules:
  0.0 70.4 jit_solution(12872749209496900425)
XLA Ops:
  0.6 0.0 copy-start
  0.6 1.6 %shard_map.94 = bf16[64,16,128]{2,1,0:T(8,128)(2,1)} custom-call(bf16[64,8,128]{2,1,0:T(8,128)(2,1)} %bitcast.9, bf16[64,8,128]{2,1,0:T(8,128)(2,1)} %bitcast.10), custom_call_target="tpu_custom_call" | custom-call | tf_op jit(solution)/shard_map/pallas_call | solution.py:263
  2.3 10.7 %all-to-all-start = ((bf16[64,16,128]{2,1,0:T(8,128)(2,1)}), bf16[64,16,128]{2,1,0:T(8,128)(2,1)S(1)}, u32[]{:S(2)}, u32[]{:S(2)}) async-start(bf16[64,16,128]{2,1,0:T(8,128)(2,1)} %shard_map.94), calls=%async_computation | async-start | bytes 524288 | tf_op jit(solution)/shard_map/all_to_all | solution.py:273
  13.0 0.1 rev.8
  13.1 0.1 rev.7
  13.2 0.8 %dynamic-slice_negate_fusion = f32[8]{0:T(128)S(1)} fusion(f32[512]{0:T(512)} %param.10, s32[]{:T(128)S(6)} %select_n.33), kind=kLoop, calls=%fused_computation.17 | loop fusion | flops 8 | bytes 68 | tf_op jit(solution)/shard_map/neg | solution.py:192
  14.0 0.1 multiply_exponential_fusion.fall_ref
  14.1 0.1 multiply_exponential_fusion.2
  14.1 0.0 copy-done
  14.1 0.1 constant_dynamic-slice_fusion
  14.2 0.1 copy.13
  14.3 0.1 maximum_bitcast_fusion
  14.4 0.8 %pad_maximum_fusion.3 = (f32[128]{0:T(128)S(1)}, f32[128]{0:T(128)S(1)}) fusion(f32[64]{0:T(128)} %param.11, f32[64]{0:T(128)} %param.12), kind=kLoop, calls=%fused_computation.15 | loop fusion | flops 256 | bytes 1536 | tf_op jit(solution)/shard_map/concatenate | solution.py:183
  15.2 0.5 fusion
  15.8 0.1 multiply_exponential_fusion.1.rise_ref
  15.9 0.3 cosine_select_fusion.turn_ref
  16.2 0.0 copy-start.1
  16.2 0.8 %copy-done.1 = f32[512,32]{0,1:T(8,128)S(1)} copy-done((f32[512,32]{0,1:T(8,128)S(1)}, f32[512,32]{0,1:T(8,128)}, u32[]{:S(2)}) %copy-start.1) | copy-done | bytes 65560
  17.0 0.8 %shard_map.95 = (bf16[8,2,8,64,128]{4,3,2,1,0:T(8,128)(2,1)S(1)}, f32[8,64,128]{2,1,0:T(8,128)S(1)}, bf16[8,128,256]{2,1,0:T(8,128)(2,1)S(1)}, bf16[128,256]{1,0:T(8,128)(2,1)S(1)}, bf16[96,512]{1,0:T(8,128)(2,1)S(1)}) custom-call(f32[2,64,128]{2,1,0:T(8,128)S(1)} %cosine_select_fusion.turn_ref, f32[2,128,128]{2,1,0:T(8,128)S(1)} %pad_maximum_fusion.wave_ref, ...), custom_call_target="tpu_custom_call" | custom-call | tf_op jit(solution)/shard_map/pallas_call | solution.py:195
  17.9 7.3 %all-to-all-done.got_ref = bf16[64,16,128]{2,1,0:T(8,128)(2,1)S(1)} async-done(((bf16[64,16,128]{2,1,0:T(8,128)(2,1)}), bf16[64,16,128]{2,1,0:T(8,128)(2,1)S(1)}, u32[]{:S(2)}, u32[]{:S(2)}) %all-to-all-start) | async-done | bytes 262176 | tf_op jit(solution)/shard_map/all_to_all | solution.py:273
  25.2 4.1 %shard_map.96 = bf16[64,24,128]{2,1,0:T(8,128)(2,1)S(1)} custom-call(bf16[64,16,128]{2,1,0:T(8,128)(2,1)S(1)} %all-to-all-done.got_ref, bf16[8,2,8,64,128]{4,3,2,1,0:T(8,128)(2,1)S(1)} %get-tuple-element.11.filt_ref, f32[8,64,128]{2,1,0:T(8,128)S(1)} %get-tuple-element.12.turn_ref, bf16[8,128,256]{2,1,0:T(8,128)(2,1)S(1)} %get-tuple-element.13.wave_ref, ...), custom_call_target="tpu_custom_call" | custom-call | tf_op jit(solution)/shard_map/pallas_call | solution.py:115
  29.3 20.2 %all_to_all.15.home_ref = bf16[64,24,128]{2,1,0:T(8,128)(2,1)S(1)} all-to-all(bf16[64,24,128]{2,1,0:T(8,128)(2,1)S(1)} %shard_map.96), channel_id=1, replica_groups=mesh['seq'=64,'chan'=8] {'seq'}, dimensions={0} | all-to-all | bytes 786432 | tf_op jit(solution)/shard_map/all_to_all | solution.py:280
  49.5 0.7 %shard_map.97 = (bf16[64,8,128]{2,1,0:T(8,128)(2,1)}, bf16[64,8,128]{2,1,0:T(8,128)(2,1)}, f32[8,32,128]{2,1,0:T(8,128)S(1)}) custom-call(bf16[64,24,128]{2,1,0:T(8,128)(2,1)S(1)} %all_to_all.15.home_ref, bf16[96,512]{1,0:T(8,128)(2,1)S(1)} %get-tuple-element.15.rows_ref), custom_call_target="tpu_custom_call" | custom-call | tf_op jit(solution)/shard_map/pallas_call | solution.py:282
  50.2 19.5 %all_to_all.16 = f32[8,32,128]{2,1,0:T(8,128)S(1)} all-to-all(f32[8,32,128]{2,1,0:T(8,128)S(1)} %get-tuple-element.18), channel_id=1, replica_groups=mesh['seq'=64,'chan'=8] {'chan'}, dimensions={0} | all-to-all | bytes 262144 | tf_op jit(solution)/shard_map/all_to_all | solution.py:295
  69.8 0.6 slice_reduce_fusion
  (7 shorter events, 0.0 us)
Async XLA Ops:
  0.6 13.5 %copy-start = (f32[512,64]{0,1:T(8,128)S(1)}, f32[512,64]{0,1:T(8,128)}, u32[]{:S(2)}) copy-start(f32[512,64]{0,1:T(8,128)} %param.9) | copy-start | bytes 393220
  2.3 22.9 %all-to-all-start = ((bf16[64,16,128]{2,1,0:T(8,128)(2,1)}), bf16[64,16,128]{2,1,0:T(8,128)(2,1)S(1)}, u32[]{:S(2)}, u32[]{:S(2)}) async-start(bf16[64,16,128]{2,1,0:T(8,128)(2,1)} %shard_map.94), calls=%async_computation | async-start | bytes 524288 | tf_op jit(solution)/shard_map/all_to_all | solution.py:273
  16.2 0.8 %copy-start.1 = (f32[512,32]{0,1:T(8,128)S(1)}, f32[512,32]{0,1:T(8,128)}, u32[]{:S(2)}) copy-start(f32[512,32]{0,1:T(8,128)} %param.13) | copy-start | bytes 196612

commit v8 on v5

--- a/solution.py
+++ b/solution.py
@@ -8,7 +8,7 @@
 from jax.sharding import PartitionSpec as P
 
 LANES = 128
-GROUP = 4
+GROUP = 8
 CHUNKS = 4
 
 highest = lax.Precision.HIGHEST

time: 70.8 us -> 70.8 us (level)
  no operation moved by 1% of the time
where the time goes in v8:
time: 70.8 us; the launch traced here: 70.5 us
  blocking collectives  39.7 us (56%)
  starting transfers between devices  10.7 us (15%)
  waiting for transfers between devices  8.17 us (12%)
  Pallas kernels  7.39 us (10%)
  other arithmetic  3.42 us (5%)
  between operations  0.76 us (1%)
    all_to_all x1, blocking collectives, per_device(): home = lax.all_to_all(back, 'seq', split_axis=0, concat_axis=0, tiled=True)  20.2 us
    all_to_all x1, blocking collectives, per_device(): lax.all_to_all(everyone, 'chan', split_axis=0, concat_axis=0, tiled=True)  19.5 us
    all_to_all x1, starting transfers between devices, per_device(): got = lax.all_to_all(sent, 'seq', split_axis=0, concat_axis=0, tiled=True)  10.7 us
    all_to_all x1, waiting for transfers between devices, per_device(): got = lax.all_to_all(sent, 'seq', split_axis=0, concat_axis=0, tiled=True)  8.17 us
    pallas_call x1, Pallas kernels, run_slab(): pl.pallas_call(slab_kernel, out_shape=jax.ShapeDtypeStruct((blocks, 3 * c...  4.12 us
    pallas_call x1, Pallas kernels, per_device(): pl.pallas_call(pack_kernel, out_shape=jax.ShapeDtypeStruct((groups, 2 * c...  1.64 us
  transfers between devices with their start and end apart: 1, of which 1 were waited for; matrix products, arithmetic and copies ran while one was open for 4% of the time, Pallas kernels for 1%

profile of v8, /device:TPU:2, one launch (start us, length us, event | category | flops | bytes accessed | tf_op | source)
XLA Modules:
  0.0 70.5 jit_solution(598199464622704568)
XLA Ops:
  0.6 0.0 copy-start
  0.6 1.6 %shard_map.94 = bf16[64,16,128]{2,1,0:T(8,128)(2,1)} custom-call(bf16[64,8,128]{2,1,0:T(8,128)(2,1)} %bitcast.9, bf16[64,8,128]{2,1,0:T(8,128)(2,1)} %bitcast.10), custom_call_target="tpu_custom_call" | custom-call | tf_op jit(solution)/shard_map/pallas_call | solution.py:252
  2.3 10.7 %all-to-all-start = ((bf16[64,16,128]{2,1,0:T(8,128)(2,1)}), bf16[64,16,128]{2,1,0:T(8,128)(2,1)S(1)}, u32[]{:S(2)}, u32[]{:S(2)}) async-start(bf16[64,16,128]{2,1,0:T(8,128)(2,1)} %shard_map.94), calls=%async_computation | async-start | bytes 524288 | tf_op jit(solution)/shard_map/all_to_all | solution.py:262
  13.0 0.1 rev.8
  13.1 0.1 rev.7
  13.2 0.8 %dynamic-slice_negate_fusion = f32[8]{0:T(128)S(1)} fusion(f32[512]{0:T(512)} %param.10, s32[]{:T(128)S(6)} %select_n.33), kind=kLoop, calls=%fused_computation.17 | loop fusion | flops 8 | bytes 68 | tf_op jit(solution)/shard_map/neg | solution.py:184
  14.0 0.1 multiply_exponential_fusion.fall_ref
  14.1 0.1 multiply_exponential_fusion.2
  14.1 0.0 copy-done
  14.1 0.1 constant_dynamic-slice_fusion
  14.2 0.1 copy.13
  14.3 0.1 maximum_bitcast_fusion
  14.4 0.8 %pad_maximum_fusion.3 = (f32[128]{0:T(128)S(1)}, f32[128]{0:T(128)S(1)}) fusion(f32[64]{0:T(128)} %param.11, f32[64]{0:T(128)} %param.12), kind=kLoop, calls=%fused_computation.15 | loop fusion | flops 256 | bytes 1536 | tf_op jit(solution)/shard_map/concatenate | solution.py:175
  15.2 0.5 fusion
  15.8 0.1 multiply_exponential_fusion.1.rise_ref
  15.9 0.3 cosine_select_fusion.turn_ref
  16.2 0.8 %shard_map.95 = (bf16[8,2,8,64,128]{4,3,2,1,0:T(8,128)(2,1)S(1)}, f32[8,64,128]{2,1,0:T(8,128)S(1)}, bf16[8,128,256]{2,1,0:T(8,128)(2,1)S(1)}, bf16[128,256]{1,0:T(8,128)(2,1)S(1)}) custom-call(f32[2,64,128]{2,1,0:T(8,128)S(1)} %cosine_select_fusion.turn_ref, f32[2,128,128]{2,1,0:T(8,128)S(1)} %pad_maximum_fusion.wave_ref, ...), custom_call_target="tpu_custom_call" | custom-call | tf_op jit(solution)/shard_map/pallas_call | solution.py:187
  17.0 8.2 %all-to-all-done.got_ref = bf16[64,16,128]{2,1,0:T(8,128)(2,1)S(1)} async-done(((bf16[64,16,128]{2,1,0:T(8,128)(2,1)}), bf16[64,16,128]{2,1,0:T(8,128)(2,1)S(1)}, u32[]{:S(2)}, u32[]{:S(2)}) %all-to-all-start) | async-done | bytes 262176 | tf_op jit(solution)/shard_map/all_to_all | solution.py:262
  25.2 0.0 copy-start.1
  25.2 4.1 %shard_map.96 = bf16[64,24,128]{2,1,0:T(8,128)(2,1)S(1)} custom-call(bf16[64,16,128]{2,1,0:T(8,128)(2,1)S(1)} %all-to-all-done.got_ref, bf16[8,2,8,64,128]{4,3,2,1,0:T(8,128)(2,1)S(1)} %get-tuple-element.10.filt_ref, f32[8,64,128]{2,1,0:T(8,128)S(1)} %get-tuple-element.11.turn_ref, bf16[8,128,256]{2,1,0:T(8,128)(2,1)S(1)} %get-tuple-element.12.wave_ref, ...), custom_call_target="tpu_custom_call" | custom-call | tf_op jit(solution)/shard_map/pallas_call | solution.py:114
  29.3 20.2 %all_to_all.15.home_ref = bf16[64,24,128]{2,1,0:T(8,128)(2,1)S(1)} all-to-all(bf16[64,24,128]{2,1,0:T(8,128)(2,1)S(1)} %shard_map.96), channel_id=1, replica_groups=mesh['seq'=64,'chan'=8] {'seq'}, dimensions={0} | all-to-all | bytes 786432 | tf_op jit(solution)/shard_map/all_to_all | solution.py:267
  49.5 0.0 copy-done.1
  49.5 0.8 %shard_map.97 = (bf16[64,8,128]{2,1,0:T(8,128)(2,1)}, bf16[64,8,128]{2,1,0:T(8,128)(2,1)}, f32[8,32,128]{2,1,0:T(8,128)S(1)}) custom-call(bf16[64,24,128]{2,1,0:T(8,128)(2,1)S(1)} %all_to_all.15.home_ref, f32[32,512]{1,0:T(8,128)S(1)} %bitcast.8), custom_call_target="tpu_custom_call" | custom-call | tf_op jit(solution)/shard_map/pallas_call | solution.py:269
  50.3 19.5 %all_to_all.16 = f32[8,32,128]{2,1,0:T(8,128)S(1)} all-to-all(f32[8,32,128]{2,1,0:T(8,128)S(1)} %get-tuple-element.16), channel_id=1, replica_groups=mesh['seq'=64,'chan'=8] {'chan'}, dimensions={0} | all-to-all | bytes 262144 | tf_op jit(solution)/shard_map/all_to_all | solution.py:282
  69.9 0.6 slice_reduce_fusion
  (7 shorter events, 0.0 us)
Async XLA Ops:
  0.6 13.5 %copy-start = (f32[512,64]{0,1:T(8,128)S(1)}, f32[512,64]{0,1:T(8,128)}, u32[]{:S(2)}) copy-start(f32[512,64]{0,1:T(8,128)} %param.9) | copy-start | bytes 393220
  2.3 22.9 %all-to-all-start = ((bf16[64,16,128]{2,1,0:T(8,128)(2,1)}), bf16[64,16,128]{2,1,0:T(8,128)(2,1)S(1)}, u32[]{:S(2)}, u32[]{:S(2)}) async-start(bf16[64,16,128]{2,1,0:T(8,128)(2,1)} %shard_map.94), calls=%async_computation | async-start | bytes 524288 | tf_op jit(solution)/shard_map/all_to_all | solution.py:262
  25.2 24.3 %copy-start.1 = (f32[512,32]{0,1:T(8,128)S(1)}, f32[512,32]{0,1:T(8,128)}, u32[]{:S(2)}) copy-start(f32[512,32]{0,1:T(8,128)} %param.13) | copy-start | bytes 196612

commit v9 on v5

--- a/solution.py
+++ b/solution.py
@@ -9,7 +9,7 @@
 
 LANES = 128
 GROUP = 4
-CHUNKS = 4
+CHUNKS = 8
 
 highest = lax.Precision.HIGHEST
 

time: 70.8 us -> 70.9 us (level)
  no operation moved by 1% of the time
where the time goes in v9:
time: 70.9 us; the launch traced here: 70.6 us
  blocking collectives  39.7 us (56%)
  starting transfers between devices  10.7 us (15%)
  waiting for transfers between devices  8.17 us (12%)
  Pallas kernels  7.49 us (11%)
  other arithmetic  3.42 us (5%)
  between operations  0.76 us (1%)
    all_to_all x1, blocking collectives, per_device(): home = lax.all_to_all(back, 'seq', split_axis=0, concat_axis=0, tiled=True)  20.2 us
    all_to_all x1, blocking collectives, per_device(): lax.all_to_all(everyone, 'chan', split_axis=0, concat_axis=0, tiled=True)  19.5 us
    all_to_all x1, starting transfers between devices, per_device(): got = lax.all_to_all(sent, 'seq', split_axis=0, concat_axis=0, tiled=True)  10.7 us
    all_to_all x1, waiting for transfers between devices, per_device(): got = lax.all_to_all(sent, 'seq', split_axis=0, concat_axis=0, tiled=True)  8.17 us
    pallas_call x1, Pallas kernels, run_slab(): pl.pallas_call(slab_kernel, out_shape=jax.ShapeDtypeStruct((blocks, 3 * c...  4.12 us
    pallas_call x1, Pallas kernels, per_device(): pl.pallas_call(pack_kernel, out_shape=jax.ShapeDtypeStruct((groups, 2 * c...  1.74 us
  transfers between devices with their start and end apart: 1, of which 1 were waited for; matrix products, arithmetic and copies ran while one was open for 4% of the time, Pallas kernels for 1%

profile of v9, /device:TPU:2, one launch (start us, length us, event | category | flops | bytes accessed | tf_op | source)
XLA Modules:
  0.0 70.6 jit_solution(2842808459725605685)
XLA Ops:
  0.6 0.0 copy-start
  0.6 1.7 %shard_map.94 = bf16[64,16,128]{2,1,0:T(8,128)(2,1)} custom-call(bf16[64,8,128]{2,1,0:T(8,128)(2,1)} %bitcast.9, bf16[64,8,128]{2,1,0:T(8,128)(2,1)} %bitcast.10), custom_call_target="tpu_custom_call" | custom-call | tf_op jit(solution)/shard_map/pallas_call | solution.py:252
  2.4 10.7 %all-to-all-start = ((bf16[64,16,128]{2,1,0:T(8,128)(2,1)}), bf16[64,16,128]{2,1,0:T(8,128)(2,1)S(1)}, u32[]{:S(2)}, u32[]{:S(2)}) async-start(bf16[64,16,128]{2,1,0:T(8,128)(2,1)} %shard_map.94), calls=%async_computation | async-start | bytes 524288 | tf_op jit(solution)/shard_map/all_to_all | solution.py:262
  13.1 0.1 rev.8
  13.2 0.1 rev.7
  13.3 0.8 %dynamic-slice_negate_fusion = f32[8]{0:T(128)S(1)} fusion(f32[512]{0:T(512)} %param.10, s32[]{:T(128)S(6)} %select_n.33), kind=kLoop, calls=%fused_computation.17 | loop fusion | flops 8 | bytes 68 | tf_op jit(solution)/shard_map/neg | solution.py:184
  14.1 0.1 multiply_exponential_fusion.fall_ref
  14.2 0.1 multiply_exponential_fusion.2
  14.2 0.0 copy-done
  14.2 0.1 constant_dynamic-slice_fusion
  14.3 0.1 copy.13
  14.4 0.1 maximum_bitcast_fusion
  14.5 0.8 %pad_maximum_fusion.3 = (f32[128]{0:T(128)S(1)}, f32[128]{0:T(128)S(1)}) fusion(f32[64]{0:T(128)} %param.11, f32[64]{0:T(128)} %param.12), kind=kLoop, calls=%fused_computation.15 | loop fusion | flops 256 | bytes 1536 | tf_op jit(solution)/shard_map/concatenate | solution.py:175
  15.3 0.5 fusion
  15.9 0.1 multiply_exponential_fusion.1.rise_ref
  16.0 0.3 cosine_select_fusion.turn_ref
  16.3 0.8 %shard_map.95 = (bf16[8,2,8,64,128]{4,3,2,1,0:T(8,128)(2,1)S(1)}, f32[8,64,128]{2,1,0:T(8,128)S(1)}, bf16[8,128,256]{2,1,0:T(8,128)(2,1)S(1)}, bf16[128,256]{1,0:T(8,128)(2,1)S(1)}) custom-call(f32[2,64,128]{2,1,0:T(8,128)S(1)} %cosine_select_fusion.turn_ref, f32[2,128,128]{2,1,0:T(8,128)S(1)} %pad_maximum_fusion.wave_ref, ...), custom_call_target="tpu_custom_call" | custom-call | tf_op jit(solution)/shard_map/pallas_call | solution.py:187
  17.1 8.2 %all-to-all-done.got_ref = bf16[64,16,128]{2,1,0:T(8,128)(2,1)S(1)} async-done(((bf16[64,16,128]{2,1,0:T(8,128)(2,1)}), bf16[64,16,128]{2,1,0:T(8,128)(2,1)S(1)}, u32[]{:S(2)}, u32[]{:S(2)}) %all-to-all-start) | async-done | bytes 262176 | tf_op jit(solution)/shard_map/all_to_all | solution.py:262
  25.3 0.0 copy-start.1
  25.3 4.1 %shard_map.96 = bf16[64,24,128]{2,1,0:T(8,128)(2,1)S(1)} custom-call(bf16[64,16,128]{2,1,0:T(8,128)(2,1)S(1)} %all-to-all-done.got_ref, bf16[8,2,8,64,128]{4,3,2,1,0:T(8,128)(2,1)S(1)} %get-tuple-element.10.filt_ref, f32[8,64,128]{2,1,0:T(8,128)S(1)} %get-tuple-element.11.turn_ref, bf16[8,128,256]{2,1,0:T(8,128)(2,1)S(1)} %get-tuple-element.12.wave_ref, ...), custom_call_target="tpu_custom_call" | custom-call | tf_op jit(solution)/shard_map/pallas_call | solution.py:114
  29.4 20.2 %all_to_all.15.home_ref = bf16[64,24,128]{2,1,0:T(8,128)(2,1)S(1)} all-to-all(bf16[64,24,128]{2,1,0:T(8,128)(2,1)S(1)} %shard_map.96), channel_id=1, replica_groups=mesh['seq'=64,'chan'=8] {'seq'}, dimensions={0} | all-to-all | bytes 786432 | tf_op jit(solution)/shard_map/all_to_all | solution.py:267
  49.6 0.0 copy-done.1
  49.6 0.8 %shard_map.97 = (bf16[64,8,128]{2,1,0:T(8,128)(2,1)}, bf16[64,8,128]{2,1,0:T(8,128)(2,1)}, f32[8,32,128]{2,1,0:T(8,128)S(1)}) custom-call(bf16[64,24,128]{2,1,0:T(8,128)(2,1)S(1)} %all_to_all.15.home_ref, f32[32,512]{1,0:T(8,128)S(1)} %bitcast.8), custom_call_target="tpu_custom_call" | custom-call | tf_op jit(solution)/shard_map/pallas_call | solution.py:269
  50.4 19.5 %all_to_all.16 = f32[8,32,128]{2,1,0:T(8,128)S(1)} all-to-all(f32[8,32,128]{2,1,0:T(8,128)S(1)} %get-tuple-element.16), channel_id=1, replica_groups=mesh['seq'=64,'chan'=8] {'chan'}, dimensions={0} | all-to-all | bytes 262144 | tf_op jit(solution)/shard_map/all_to_all | solution.py:282
  70.0 0.6 slice_reduce_fusion
  (7 shorter events, 0.0 us)
Async XLA Ops:
  0.6 13.6 %copy-start = (f32[512,64]{0,1:T(8,128)S(1)}, f32[512,64]{0,1:T(8,128)}, u32[]{:S(2)}) copy-start(f32[512,64]{0,1:T(8,128)} %param.9) | copy-start | bytes 393220
  2.4 22.9 %all-to-all-start = ((bf16[64,16,128]{2,1,0:T(8,128)(2,1)}), bf16[64,16,128]{2,1,0:T(8,128)(2,1)S(1)}, u32[]{:S(2)}, u32[]{:S(2)}) async-start(bf16[64,16,128]{2,1,0:T(8,128)(2,1)} %shard_map.94), calls=%async_computation | async-start | bytes 524288 | tf_op jit(solution)/shard_map/all_to_all | solution.py:262
  25.3 24.3 %copy-start.1 = (f32[512,32]{0,1:T(8,128)S(1)}, f32[512,32]{0,1:T(8,128)}, u32[]{:S(2)}) copy-start(f32[512,32]{0,1:T(8,128)} %param.13) | copy-start | bytes 196612
